TPU v7x, 32 devices: a whole 2x2x4 slice. The times are simulated.
32 devices in a mesh: section: 4 (over y, x), rep: 8 (over z, core).
Axes of the slice: x: 2, y: 2, z: 4, core: 2. Of those that a mesh axis runs over, the one named last changes fastest.
Arguments:
- inputs: bfloat16 [6, 256, 6144], P(None, 'rep'), may hold values from -6 to 6
- cotangent: bfloat16 [6, 256, 6144], P(None, 'rep'), may hold values from -6 to 6
- in_weight: bfloat16 [4, 6144, 256], P('section', 'rep'), may hold values from -0.078125 to 0.078125
- out_weight: bfloat16 [4, 6144, 256], P('section', 'rep'), may hold values from -0.375 to 0.375
- norm_gain: float32 [4, 6144], P('section'), may hold values from 0.5 to 1.5
- lengths: int32 [8, 6], P('rep'), may hold values from 1 to 32, 144 in all within a row
Outputs:
- grad_in_weight: bfloat16 [4, 6144, 256], P('section', 'rep')
- grad_out_weight: bfloat16 [4, 6144, 256], P('section', 'rep')
- grad_gain: float32 [4, 6144], P('section')
- grad_inputs: bfloat16 [4, 6, 256, 6144], P('section', None, 'rep')
Inputs may be any that keep to these rules, and one draw needn't show every extreme that they name: `lengths`: each replica's 6 counts sum to 144 and the largest is 32.
All inputs are finite; a program needn't handle non-finite values.
Results may differ from a plain program's by a relative error of at most 0.025.
Values may be sent and summed in bfloat16 or wider, within the bound.
A program may use at most 64 MiB of HBM per device.

v0:
```python
import math

import jax
import jax.numpy as jnp
from jax import lax
from jax.sharding import PartitionSpec as P

norm_epsilon = 1e-05


def from_behind(block, axis, distance):
    devices = range(lax.axis_size(axis))
    route = [(i - distance, i) for i in devices if i - distance in devices]
    return lax.ppermute(block, axis, route)


def section_forward(hidden, norm_gain, in_weight, out_weight):
    widened = hidden.astype(jnp.float32)
    inverse = lax.rsqrt(jnp.mean(widened * widened, axis=-1, keepdims=True) + norm_epsilon)
    normed = (widened * inverse * norm_gain).astype(jnp.bfloat16)
    before = jnp.dot(normed, in_weight, preferred_element_type=jnp.float32)
    activated = jax.nn.silu(before).astype(jnp.bfloat16)
    mixed = lax.dot_general(
        activated, out_weight, (((1,), (1,)), ((), ())), preferred_element_type=jnp.float32
    )
    return ((widened + mixed).astype(jnp.bfloat16), normed, before, activated)


def section_backward(hidden, norm_gain, in_weight, out_weight, before, upstream):
    widened = hidden.astype(jnp.float32)
    inverse = lax.rsqrt(jnp.mean(widened * widened, axis=-1, keepdims=True) + norm_epsilon)
    grad_activated = jnp.dot(upstream, out_weight, preferred_element_type=jnp.float32)
    sigmoid_value = jax.nn.sigmoid(before)
    grad_before = (grad_activated * sigmoid_value * (1.0 + before * (1.0 - sigmoid_value))).astype(
        jnp.bfloat16
    )
    grad_normed = lax.dot_general(
        grad_before, in_weight, (((1,), (1,)), ((), ())), preferred_element_type=jnp.float32
    )
    grad_scaled = grad_normed * norm_gain
    projection = jnp.mean(grad_scaled * widened, axis=-1, keepdims=True)
    grad_hidden = (
        upstream.astype(jnp.float32)
        + inverse * grad_scaled
        - widened * (inverse * inverse * inverse) * projection
    )
    gain_terms = jnp.sum(grad_normed * widened * inverse, axis=0)
    return (grad_hidden.astype(jnp.bfloat16), grad_before, gain_terms)


def write_slot(holders, contents, slot):
    return tuple(
        (
            lax.dynamic_update_index_in_dim(holder, content, slot, 0)
            for holder, content in zip(holders, contents)
        )
    )


def body(inputs, cotangent, in_weight, out_weight, norm_gain, lengths):
    section_count = lax.axis_size("section")
    replicas = lax.axis_size("rep")
    position = lax.axis_index("section")
    micro_count, tok_rows, width = inputs.shape
    grad_scale = 1.0 / math.sqrt(micro_count * tok_rows * replicas)
    gain_row = norm_gain[0]
    full_in, full_out = (
        lax.all_gather(in_weight[0], "rep", axis=0, tiled=True),
        lax.all_gather(out_weight[0], "rep", axis=0, tiled=True),
    )
    rank_width = full_in.shape[1]
    tick_total = micro_count + section_count - 1
    blank = jnp.zeros((tok_rows, width), jnp.bfloat16)
    wide_zeros = jnp.zeros((micro_count, tok_rows, width), jnp.bfloat16)
    narrow_zeros = jnp.zeros((micro_count, tok_rows, rank_width), jnp.bfloat16)
    stores = (wide_zeros,)

    def forward_tick(moment, carried):
        received, holders = carried
        micro = moment - position
        active = (micro >= 0) & (micro < micro_count)
        slot = jnp.clip(micro, 0, micro_count - 1)
        fresh = lax.dynamic_index_in_dim(inputs, slot, 0, keepdims=False)
        entering = jnp.where(position == 0, fresh, received)

        def forward_run_section(holders):
            leaving, normed, before, activated = section_forward(
                entering, gain_row, full_in, full_out
            )
            contents = (entering,)
            return (leaving, write_slot(holders, contents, slot))

        def forward_skip_section(holders):
            return (blank, holders)

        leaving, holders = lax.cond(active, forward_run_section, forward_skip_section, holders)
        received = from_behind(leaving, "section", 1)
        return (received, holders)

    received, stores = lax.fori_loop(0, tick_total, forward_tick, (blank, stores))
    keep_rows = jnp.arange(tok_rows, dtype=jnp.int32)[None, :] < lengths[0][:, None]
    seeds = jnp.where(keep_rows[:, :, None], cotangent, jnp.zeros((), jnp.bfloat16))
    gain_start = jnp.zeros((width,), jnp.float32)
    buffers = (wide_zeros, narrow_zeros, wide_zeros, wide_zeros, narrow_zeros)

    def backward_tick(moment, carried):
        received, holders, gain_total = carried
        micro = moment - (section_count - 1 - position)
        active = (micro >= 0) & (micro < micro_count)
        slot = jnp.clip(micro, 0, micro_count - 1)
        seed_rows = lax.dynamic_index_in_dim(seeds, slot, 0, keepdims=False)
        entering = jnp.where(position == section_count - 1, seed_rows, received)

        def backward_run_section(operands):
            holders, gain_total = operands
            hidden_rows = lax.dynamic_index_in_dim(stores[0], slot, 0, keepdims=False)
            unused, normed, before, activated = section_forward(
                hidden_rows, gain_row, full_in, full_out
            )
            grad_hidden, grad_before, gain_terms = section_backward(
                hidden_rows, gain_row, full_in, full_out, before, entering
            )
            contents = (grad_hidden, grad_before, entering, normed, activated)
            return (grad_hidden, (write_slot(holders, contents, slot), gain_total + gain_terms))

        def backward_skip_section(operands):
            return (blank, operands)

        leaving, (holders, gain_total) = lax.cond(
            active, backward_run_section, backward_skip_section, (holders, gain_total)
        )
        received = from_behind(leaving, "section", -1)
        return (received, holders, gain_total)

    received, buffers, gain_total = lax.fori_loop(
        0, tick_total, backward_tick, (blank, buffers, gain_start)
    )
    normed_all = buffers[3]
    activated_all = buffers[4]
    flat_rows = micro_count * tok_rows
    normed_flat = normed_all.reshape(flat_rows, width)
    upstream_flat = buffers[2].reshape(flat_rows, width)
    before_flat = buffers[1].reshape(flat_rows, rank_width)
    activated_flat = activated_all.reshape(flat_rows, rank_width)
    left_term = lax.dot_general(
        normed_flat, before_flat, (((0,), (0,)), ((), ())), preferred_element_type=jnp.float32
    )
    right_term = lax.dot_general(
        upstream_flat, activated_flat, (((0,), (0,)), ((), ())), preferred_element_type=jnp.float32
    )
    summed = lax.psum_scatter(
        (jnp.concatenate((left_term, right_term), axis=1) * grad_scale).astype(jnp.bfloat16),
        "rep",
        scatter_dimension=0,
        tiled=True,
    ).astype(jnp.float32)
    grad_in_weight = summed[:, :rank_width].astype(jnp.bfloat16)[None]
    grad_out_weight = summed[:, rank_width:].astype(jnp.bfloat16)[None]
    grad_gain = lax.psum(gain_total * grad_scale, "rep")[None]
    grad_inputs = buffers[0][None]
    return (grad_in_weight, grad_out_weight, grad_gain, grad_inputs)


def solution(mesh):
    in_specs = (
        P(None, "rep", None),
        P(None, "rep", None),
        P("section", "rep", None),
        P("section", "rep", None),
        P("section", None),
        P("rep", None),
    )
    out_specs = (
        P("section", "rep", None),
        P("section", "rep", None),
        P("section", None),
        P("section", None, "rep", None),
    )
    return jax.shard_map(body, mesh=mesh, in_specs=in_specs, out_specs=out_specs, check_vma=False)
```

profile of v0, /device:TPU:0, one launch (start us, length us, event | category | flops | bytes accessed | tf_op | source)
XLA Modules:
  0.0 532.2 jit_solution(10388793744136409346)
XLA Ops:
  9.4 3.4 broadcast_select_fusion
  12.8 37.8 %all-gather.5.cloned.1.call-done = bf16[1,6144,256]{2,1,0:T(8,128)(2,1)} async-done(((bf16[1,768,256]{2,1,0:T(8,128)(2,1)}), bf16[1,6144,256]{2,1,0:T(8,128)(2,1)}) %all-gather.5.cloned.1.call-update) | async-done | bytes 3145744 | tf_op jit(solution)/shard_map/all_gather | solution.py:68
  50.6 38.8 %all-gather.7.cloned.1.call-done = bf16[1,6144,256]{2,1,0:T(8,128)(2,1)} async-done(((bf16[1,768,256]{2,1,0:T(8,128)(2,1)}), bf16[1,6144,256]{2,1,0:T(8,128)(2,1)}) %all-gather.7.cloned.1.call-update) | async-done | bytes 3145744 | tf_op jit(solution)/shard_map/all_gather | solution.py:69
  89.7 159.5 %while.46 = (s32[]{:T(128)}, bf16[32,6144]{1,0:T(8,128)(2,1)S(1)}, bf16[6,32,6144]{2,1,0:T(8,128)(2,1)S(1)}, s32[]{:T(128)}, pred[]{:T(512)}, /*index=5*/bf16[6,...) while((s32[]{:T(128)}, bf16[32,6144]{1,0:T(8,128)(2,1)S(1)}, ...), condition=%wide.region_4.5_spmd, body=%wide.region_0.4_spmd.sunk | while | flops 203530272 | bytes 12215116 | solution.py:100
  89.7 6.5 %conditional.4 = (bf16[32,6144]{1,0:T(8,128)(2,1)S(1)}, bf16[6,32,6144]{2,1,0:T(8,128)(2,1)S(1)}) conditional(s32[]{:T(128)} %convert_element_type.183, bf16[6,32,6144]{2,1,0:T(8,128)(2,1)S(1)} %get-tuple-element.1063, (pred[]{:T(512)}, s32[]{:T(128)}, bf16[6,32,6144]{2,1,0:T(8,128)(2,1)}, bf16[32,6144]{1,0:T(8,128)(2,1)S(1)}, ...), branch_computations={%region_1.1_spmd, %region_2.3_spmd} | conditional | flops 203530272 | bytes 9069101 | solution.py:96
  91.1 5.2 fusion
  98.3 9.3 %collective-permute-done = bf16[32,6144]{1,0:T(8,128)(2,1)S(1)} collective-permute-done((bf16[32,6144]{1,0:T(8,128)(2,1)}, bf16[32,6144]{1,0:T(8,128)(2,1)S(1)}, u32[]{:S(2)}, u32[]{:S(2)}) %collective-permute-start) | collective-permute-done | bytes 393248 | tf_op jit(solution)/shard_map/while/body/eval_jaxpr/ppermute | solution.py:14
  107.6 6.5 %conditional.4 = (bf16[32,6144]{1,0:T(8,128)(2,1)S(1)}, bf16[6,32,6144]{2,1,0:T(8,128)(2,1)S(1)}) conditional(s32[]{:T(128)} %convert_element_type.183, bf16[6,32,6144]{2,1,0:T(8,128)(2,1)S(1)} %get-tuple-element.1063, (pred[]{:T(512)}, s32[]{:T(128)}, bf16[6,32,6144]{2,1,0:T(8,128)(2,1)}, bf16[32,6144]{1,0:T(8,128)(2,1)S(1)}, ...), branch_computations={%region_1.1_spmd, %region_2.3_spmd} | conditional | flops 203530272 | bytes 9069101 | solution.py:96
  108.9 5.1 fusion
  114.8 4.3 collective-permute-start
  119.2 8.5 %collective-permute-done = bf16[32,6144]{1,0:T(8,128)(2,1)S(1)} collective-permute-done((bf16[32,6144]{1,0:T(8,128)(2,1)}, bf16[32,6144]{1,0:T(8,128)(2,1)S(1)}, u32[]{:S(2)}, u32[]{:S(2)}) %collective-permute-start) | collective-permute-done | bytes 393248 | tf_op jit(solution)/shard_map/while/body/eval_jaxpr/ppermute | solution.py:14
  127.6 6.5 %conditional.4 = (bf16[32,6144]{1,0:T(8,128)(2,1)S(1)}, bf16[6,32,6144]{2,1,0:T(8,128)(2,1)S(1)}) conditional(s32[]{:T(128)} %convert_element_type.183, bf16[6,32,6144]{2,1,0:T(8,128)(2,1)S(1)} %get-tuple-element.1063, (pred[]{:T(512)}, s32[]{:T(128)}, bf16[6,32,6144]{2,1,0:T(8,128)(2,1)}, bf16[32,6144]{1,0:T(8,128)(2,1)S(1)}, ...), branch_computations={%region_1.1_spmd, %region_2.3_spmd} | conditional | flops 203530272 | bytes 9069101 | solution.py:96
  128.9 5.2 fusion
  134.9 4.3 collective-permute-start
  139.2 7.6 %collective-permute-done = bf16[32,6144]{1,0:T(8,128)(2,1)S(1)} collective-permute-done((bf16[32,6144]{1,0:T(8,128)(2,1)}, bf16[32,6144]{1,0:T(8,128)(2,1)S(1)}, u32[]{:S(2)}, u32[]{:S(2)}) %collective-permute-start) | collective-permute-done | bytes 393248 | tf_op jit(solution)/shard_map/while/body/eval_jaxpr/ppermute | solution.py:14
  146.8 6.5 %conditional.4 = (bf16[32,6144]{1,0:T(8,128)(2,1)S(1)}, bf16[6,32,6144]{2,1,0:T(8,128)(2,1)S(1)}) conditional(s32[]{:T(128)} %convert_element_type.183, bf16[6,32,6144]{2,1,0:T(8,128)(2,1)S(1)} %get-tuple-element.1063, (pred[]{:T(512)}, s32[]{:T(128)}, bf16[6,32,6144]{2,1,0:T(8,128)(2,1)}, bf16[32,6144]{1,0:T(8,128)(2,1)S(1)}, ...), branch_computations={%region_1.1_spmd, %region_2.3_spmd} | conditional | flops 203530272 | bytes 9069101 | solution.py:96
  148.1 5.2 fusion
  154.0 4.3 collective-permute-start
  158.3 6.8 %collective-permute-done = bf16[32,6144]{1,0:T(8,128)(2,1)S(1)} collective-permute-done((bf16[32,6144]{1,0:T(8,128)(2,1)}, bf16[32,6144]{1,0:T(8,128)(2,1)S(1)}, u32[]{:S(2)}, u32[]{:S(2)}) %collective-permute-start) | collective-permute-done | bytes 393248 | tf_op jit(solution)/shard_map/while/body/eval_jaxpr/ppermute | solution.py:14
  165.1 6.5 %conditional.4 = (bf16[32,6144]{1,0:T(8,128)(2,1)S(1)}, bf16[6,32,6144]{2,1,0:T(8,128)(2,1)S(1)}) conditional(s32[]{:T(128)} %convert_element_type.183, bf16[6,32,6144]{2,1,0:T(8,128)(2,1)S(1)} %get-tuple-element.1063, (pred[]{:T(512)}, s32[]{:T(128)}, bf16[6,32,6144]{2,1,0:T(8,128)(2,1)}, bf16[32,6144]{1,0:T(8,128)(2,1)S(1)}, ...), branch_computations={%region_1.1_spmd, %region_2.3_spmd} | conditional | flops 203530272 | bytes 9069101 | solution.py:96
  166.4 5.2 fusion
  172.3 4.5 collective-permute-start
  176.9 6.2 %collective-permute-done = bf16[32,6144]{1,0:T(8,128)(2,1)S(1)} collective-permute-done((bf16[32,6144]{1,0:T(8,128)(2,1)}, bf16[32,6144]{1,0:T(8,128)(2,1)S(1)}, u32[]{:S(2)}, u32[]{:S(2)}) %collective-permute-start) | collective-permute-done | bytes 393248 | tf_op jit(solution)/shard_map/while/body/eval_jaxpr/ppermute | solution.py:14
  183.0 6.5 %conditional.4 = (bf16[32,6144]{1,0:T(8,128)(2,1)S(1)}, bf16[6,32,6144]{2,1,0:T(8,128)(2,1)S(1)}) conditional(s32[]{:T(128)} %convert_element_type.183, bf16[6,32,6144]{2,1,0:T(8,128)(2,1)S(1)} %get-tuple-element.1063, (pred[]{:T(512)}, s32[]{:T(128)}, bf16[6,32,6144]{2,1,0:T(8,128)(2,1)}, bf16[32,6144]{1,0:T(8,128)(2,1)S(1)}, ...), branch_computations={%region_1.1_spmd, %region_2.3_spmd} | conditional | flops 203530272 | bytes 9069101 | solution.py:96
  184.3 5.2 fusion
  190.3 5.2 collective-permute-start
  195.5 5.6 %collective-permute-done = bf16[32,6144]{1,0:T(8,128)(2,1)S(1)} collective-permute-done((bf16[32,6144]{1,0:T(8,128)(2,1)}, bf16[32,6144]{1,0:T(8,128)(2,1)S(1)}, u32[]{:S(2)}, u32[]{:S(2)}) %collective-permute-start) | collective-permute-done | bytes 393248 | tf_op jit(solution)/shard_map/while/body/eval_jaxpr/ppermute | solution.py:14
  201.8 11.7 %collective-permute-start = (bf16[32,6144]{1,0:T(8,128)(2,1)}, bf16[32,6144]{1,0:T(8,128)(2,1)S(1)}, u32[]{:S(2)}, u32[]{:S(2)}) collective-permute-start(bf16[32,6144]{1,0:T(8,128)(2,1)} %copy-done.5), channel_id=1, source_target_pairs={{0,8},{8,16},{16,24},{1,9},{9,17},{17,25},{2,10},{10,18},{18,26},{... | collective-permute-start | bytes 1179656 | tf_op jit(solution)/shard_map/while/body/eval_jaxpr/ppermute | solution.py:14
  213.5 5.6 %collective-permute-done = bf16[32,6144]{1,0:T(8,128)(2,1)S(1)} collective-permute-done((bf16[32,6144]{1,0:T(8,128)(2,1)}, bf16[32,6144]{1,0:T(8,128)(2,1)S(1)}, u32[]{:S(2)}, u32[]{:S(2)}) %collective-permute-start) | collective-permute-done | bytes 393248 | tf_op jit(solution)/shard_map/while/body/eval_jaxpr/ppermute | solution.py:14
  219.8 5.2 collective-permute-start
  225.0 5.6 %collective-permute-done = bf16[32,6144]{1,0:T(8,128)(2,1)S(1)} collective-permute-done((bf16[32,6144]{1,0:T(8,128)(2,1)}, bf16[32,6144]{1,0:T(8,128)(2,1)S(1)}, u32[]{:S(2)}, u32[]{:S(2)}) %collective-permute-start) | collective-permute-done | bytes 393248 | tf_op jit(solution)/shard_map/while/body/eval_jaxpr/ppermute | solution.py:14
  231.4 12.2 %collective-permute-start = (bf16[32,6144]{1,0:T(8,128)(2,1)}, bf16[32,6144]{1,0:T(8,128)(2,1)S(1)}, u32[]{:S(2)}, u32[]{:S(2)}) collective-permute-start(bf16[32,6144]{1,0:T(8,128)(2,1)} %copy-done.5), channel_id=1, source_target_pairs={{0,8},{8,16},{16,24},{1,9},{9,17},{17,25},{2,10},{10,18},{18,26},{... | collective-permute-start | bytes 1179656 | tf_op jit(solution)/shard_map/while/body/eval_jaxpr/ppermute | solution.py:14
  243.6 5.6 %collective-permute-done = bf16[32,6144]{1,0:T(8,128)(2,1)S(1)} collective-permute-done((bf16[32,6144]{1,0:T(8,128)(2,1)}, bf16[32,6144]{1,0:T(8,128)(2,1)S(1)}, u32[]{:S(2)}, u32[]{:S(2)}) %collective-permute-start) | collective-permute-done | bytes 393248 | tf_op jit(solution)/shard_map/while/body/eval_jaxpr/ppermute | solution.py:14
  255.9 191.4 %while.47 = (s32[]{:T(128)}, bf16[32,6144]{1,0:T(8,128)(2,1)}, bf16[6,32,6144]{2,1,0:T(8,128)(2,1)}, bf16[6,32,256]{2,1,0:T(8,128)(2,1)S(1)}, bf16[6,32,6144]{2,...) while((s32[]{:T(128)}, bf16[32,6144]{1,0:T(8,128)(2,1)}, ...), condition=%wide.region_11.12_spmd, body=%wide.region_5.11_spmd.sunk | while | flops 307413088 | bytes 30610964 | solution.py:135
  257.9 9.9 %collective-permute-done.1 = bf16[32,6144]{1,0:T(8,128)(2,1)} collective-permute-done((bf16[32,6144]{1,0:T(8,128)(2,1)}, bf16[32,6144]{1,0:T(8,128)(2,1)}, u32[]{:S(2)}, u32[]{:S(2)}) %collective-permute-start.1) | collective-permute-done | bytes 393248 | tf_op jit(solution)/shard_map/while/body/eval_jaxpr/ppermute | solution.py:14
  269.9 11.7 %collective-permute-done.1 = bf16[32,6144]{1,0:T(8,128)(2,1)} collective-permute-done((bf16[32,6144]{1,0:T(8,128)(2,1)}, bf16[32,6144]{1,0:T(8,128)(2,1)}, u32[]{:S(2)}, u32[]{:S(2)}) %collective-permute-start.1) | collective-permute-done | bytes 393248 | tf_op jit(solution)/shard_map/while/body/eval_jaxpr/ppermute | solution.py:14
  283.7 36.6 %collective-permute-done.1 = bf16[32,6144]{1,0:T(8,128)(2,1)} collective-permute-done((bf16[32,6144]{1,0:T(8,128)(2,1)}, bf16[32,6144]{1,0:T(8,128)(2,1)}, u32[]{:S(2)}, u32[]{:S(2)}) %collective-permute-start.1) | collective-permute-done | bytes 393248 | tf_op jit(solution)/shard_map/while/body/eval_jaxpr/ppermute | solution.py:14
  320.3 10.2 %conditional.5 = (bf16[32,6144]{1,0:T(8,128)(2,1)}, bf16[6,32,6144]{2,1,0:T(8,128)(2,1)}, bf16[6,32,256]{2,1,0:T(8,128)(2,1)S(1)}, bf16[6,32,6144]{2,1,0:T(8,128...) conditional(s32[]{:T(128)} %convert_element_type.184, ...), branch_computations={%region_6.6_spmd, %region_7.10_spmd} | conditional | flops 307413088 | bytes 29037696 | solution.py:129
  326.0 2.2 fusion.29
  328.2 2.3 bitcast_dynamic-update-slice_fusion.2
  331.8 9.6 %collective-permute-done.1 = bf16[32,6144]{1,0:T(8,128)(2,1)} collective-permute-done((bf16[32,6144]{1,0:T(8,128)(2,1)}, bf16[32,6144]{1,0:T(8,128)(2,1)}, u32[]{:S(2)}, u32[]{:S(2)}) %collective-permute-start.1) | collective-permute-done | bytes 393248 | tf_op jit(solution)/shard_map/while/body/eval_jaxpr/ppermute | solution.py:14
  341.4 10.2 %conditional.5 = (bf16[32,6144]{1,0:T(8,128)(2,1)}, bf16[6,32,6144]{2,1,0:T(8,128)(2,1)}, bf16[6,32,256]{2,1,0:T(8,128)(2,1)S(1)}, bf16[6,32,6144]{2,1,0:T(8,128...) conditional(s32[]{:T(128)} %convert_element_type.184, ...), branch_computations={%region_6.6_spmd, %region_7.10_spmd} | conditional | flops 307413088 | bytes 29037696 | solution.py:129
  347.1 2.2 fusion.29
  349.3 2.3 bitcast_dynamic-update-slice_fusion.2
  352.9 9.6 %collective-permute-done.1 = bf16[32,6144]{1,0:T(8,128)(2,1)} collective-permute-done((bf16[32,6144]{1,0:T(8,128)(2,1)}, bf16[32,6144]{1,0:T(8,128)(2,1)}, u32[]{:S(2)}, u32[]{:S(2)}) %collective-permute-start.1) | collective-permute-done | bytes 393248 | tf_op jit(solution)/shard_map/while/body/eval_jaxpr/ppermute | solution.py:14
  362.5 10.2 %conditional.5 = (bf16[32,6144]{1,0:T(8,128)(2,1)}, bf16[6,32,6144]{2,1,0:T(8,128)(2,1)}, bf16[6,32,256]{2,1,0:T(8,128)(2,1)S(1)}, bf16[6,32,6144]{2,1,0:T(8,128...) conditional(s32[]{:T(128)} %convert_element_type.184, ...), branch_computations={%region_6.6_spmd, %region_7.10_spmd} | conditional | flops 307413088 | bytes 29037696 | solution.py:129
  368.2 2.2 fusion.29
  370.4 2.3 bitcast_dynamic-update-slice_fusion.2
  374.0 9.6 %collective-permute-done.1 = bf16[32,6144]{1,0:T(8,128)(2,1)} collective-permute-done((bf16[32,6144]{1,0:T(8,128)(2,1)}, bf16[32,6144]{1,0:T(8,128)(2,1)}, u32[]{:S(2)}, u32[]{:S(2)}) %collective-permute-start.1) | collective-permute-done | bytes 393248 | tf_op jit(solution)/shard_map/while/body/eval_jaxpr/ppermute | solution.py:14
  383.6 10.3 %conditional.5 = (bf16[32,6144]{1,0:T(8,128)(2,1)}, bf16[6,32,6144]{2,1,0:T(8,128)(2,1)}, bf16[6,32,256]{2,1,0:T(8,128)(2,1)S(1)}, bf16[6,32,6144]{2,1,0:T(8,128...) conditional(s32[]{:T(128)} %convert_element_type.184, ...), branch_computations={%region_6.6_spmd, %region_7.10_spmd} | conditional | flops 307413088 | bytes 29037696 | solution.py:129
  389.4 2.2 fusion.29
  391.6 2.3 bitcast_dynamic-update-slice_fusion.2
  395.2 9.6 %collective-permute-done.1 = bf16[32,6144]{1,0:T(8,128)(2,1)} collective-permute-done((bf16[32,6144]{1,0:T(8,128)(2,1)}, bf16[32,6144]{1,0:T(8,128)(2,1)}, u32[]{:S(2)}, u32[]{:S(2)}) %collective-permute-start.1) | collective-permute-done | bytes 393248 | tf_op jit(solution)/shard_map/while/body/eval_jaxpr/ppermute | solution.py:14
  404.8 10.3 %conditional.5 = (bf16[32,6144]{1,0:T(8,128)(2,1)}, bf16[6,32,6144]{2,1,0:T(8,128)(2,1)}, bf16[6,32,256]{2,1,0:T(8,128)(2,1)S(1)}, bf16[6,32,6144]{2,1,0:T(8,128...) conditional(s32[]{:T(128)} %convert_element_type.184, ...), branch_computations={%region_6.6_spmd, %region_7.10_spmd} | conditional | flops 307413088 | bytes 29037696 | solution.py:129
  412.7 2.3 bitcast_dynamic-update-slice_fusion.2
  416.3 10.7 %collective-permute-done.1 = bf16[32,6144]{1,0:T(8,128)(2,1)} collective-permute-done((bf16[32,6144]{1,0:T(8,128)(2,1)}, bf16[32,6144]{1,0:T(8,128)(2,1)}, u32[]{:S(2)}, u32[]{:S(2)}) %collective-permute-start.1) | collective-permute-done | bytes 393248 | tf_op jit(solution)/shard_map/while/body/eval_jaxpr/ppermute | solution.py:14
  427.0 10.3 %conditional.5 = (bf16[32,6144]{1,0:T(8,128)(2,1)}, bf16[6,32,6144]{2,1,0:T(8,128)(2,1)}, bf16[6,32,256]{2,1,0:T(8,128)(2,1)S(1)}, bf16[6,32,6144]{2,1,0:T(8,128...) conditional(s32[]{:T(128)} %convert_element_type.184, ...), branch_computations={%region_6.6_spmd, %region_7.10_spmd} | conditional | flops 307413088 | bytes 29037696 | solution.py:129
  432.8 2.2 fusion.29
  435.0 2.3 bitcast_dynamic-update-slice_fusion.2
  438.6 8.7 %collective-permute-done.1 = bf16[32,6144]{1,0:T(8,128)(2,1)} collective-permute-done((bf16[32,6144]{1,0:T(8,128)(2,1)}, bf16[32,6144]{1,0:T(8,128)(2,1)}, u32[]{:S(2)}, u32[]{:S(2)}) %collective-permute-start.1) | collective-permute-done | bytes 393248 | tf_op jit(solution)/shard_map/while/body/eval_jaxpr/ppermute | solution.py:14
  447.3 2.8 convolution_bitcast_fusion
  451.2 3.8 fusion.39
  455.0 27.8 %psum.7 = f32[1,6144]{1,0:T(1,128)} all-reduce(f32[1,6144]{1,0:T(1,128)S(1)} %bitcast.83), channel_id=1, replica_groups=mesh['section'=4,'rep'=8] {'rep'}, use_global_device_ids=true, to_apply=%region_13.14 | all-reduce | flops 6144 | bytes 49152 | tf_op jit(solution)/shard_map/psum | solution.py:159
  482.9 39.8 %reduce-scatter.2.cloned.1.call-done = bf16[768,512]{0,1:T(8,128)(2,1)} async-done(((bf16[6144,512]{0,1:T(8,128)(2,1)}), bf16[768,512]{0,1:T(8,128)(2,1)}) %reduce-scatter.2.cloned.1.call-update) | async-done | bytes 786448 | tf_op jit(solution)/shard_map/reduce_scatter | solution.py:151
  (142 shorter events, 82.0 us)
Async XLA Ops:
  7.2 43.4 %all-gather.5.cloned.1.call-start = ((), (), s32[]{:S(2)}) async-start(), calls=%async_computation.2 | async-start | bytes 3538944 | tf_op jit(solution)/shard_map/all_gather | solution.py:68
  7.9 81.5 %all-gather.7.cloned.1.call-start = ((), (), s32[]{:S(2)}) async-start(), calls=%async_computation.3 | async-start | bytes 3538944 | tf_op jit(solution)/shard_map/all_gather | solution.py:69
  8.6 514.0 %reduce-scatter.2.cloned.1.call-start = ((), (), s32[]{:S(2)}) async-start(), calls=%async_computation.1 | async-start | bytes 7077888 | tf_op jit(solution)/shard_map/reduce_scatter | solution.py:151
  12.8 76.9 %copy-start.3 = (f32[1,6144]{1,0:T(1,128)S(1)}, f32[1,6144]{1,0:T(1,128)}, u32[]{:S(2)}) copy-start(f32[1,6144]{1,0:T(1,128)} %param.18) | copy-start | bytes 73732
  96.2 0.8 copy-start.5
  97.0 10.6 %collective-permute-start = (bf16[32,6144]{1,0:T(8,128)(2,1)}, bf16[32,6144]{1,0:T(8,128)(2,1)S(1)}, u32[]{:S(2)}, u32[]{:S(2)}) collective-permute-start(bf16[32,6144]{1,0:T(8,128)(2,1)} %copy-done.5), channel_id=1, source_target_pairs={{0,8},{8,16},{16,24},{1,9},{9,17},{17,25},{2,10},{10,18},{18,26},{... | collective-permute-start | bytes 1179656 | tf_op jit(solution)/shard_map/while/body/eval_jaxpr/ppermute | solution.py:14
  114.1 0.8 copy-start.5
  114.8 12.8 %collective-permute-start = (bf16[32,6144]{1,0:T(8,128)(2,1)}, bf16[32,6144]{1,0:T(8,128)(2,1)S(1)}, u32[]{:S(2)}, u32[]{:S(2)}) collective-permute-start(bf16[32,6144]{1,0:T(8,128)(2,1)} %copy-done.5), channel_id=1, source_target_pairs={{0,8},{8,16},{16,24},{1,9},{9,17},{17,25},{2,10},{10,18},{18,26},{... | collective-permute-start | bytes 1179656 | tf_op jit(solution)/shard_map/while/body/eval_jaxpr/ppermute | solution.py:14
  134.1 0.8 copy-start.5
  134.9 11.9 %collective-permute-start = (bf16[32,6144]{1,0:T(8,128)(2,1)}, bf16[32,6144]{1,0:T(8,128)(2,1)S(1)}, u32[]{:S(2)}, u32[]{:S(2)}) collective-permute-start(bf16[32,6144]{1,0:T(8,128)(2,1)} %copy-done.5), channel_id=1, source_target_pairs={{0,8},{8,16},{16,24},{1,9},{9,17},{17,25},{2,10},{10,18},{18,26},{... | collective-permute-start | bytes 1179656 | tf_op jit(solution)/shard_map/while/body/eval_jaxpr/ppermute | solution.py:14
  153.2 0.8 copy-start.5
  154.0 11.1 %collective-permute-start = (bf16[32,6144]{1,0:T(8,128)(2,1)}, bf16[32,6144]{1,0:T(8,128)(2,1)S(1)}, u32[]{:S(2)}, u32[]{:S(2)}) collective-permute-start(bf16[32,6144]{1,0:T(8,128)(2,1)} %copy-done.5), channel_id=1, source_target_pairs={{0,8},{8,16},{16,24},{1,9},{9,17},{17,25},{2,10},{10,18},{18,26},{... | collective-permute-start | bytes 1179656 | tf_op jit(solution)/shard_map/while/body/eval_jaxpr/ppermute | solution.py:14
  171.5 0.8 copy-start.5
  172.3 10.7 %collective-permute-start = (bf16[32,6144]{1,0:T(8,128)(2,1)}, bf16[32,6144]{1,0:T(8,128)(2,1)S(1)}, u32[]{:S(2)}, u32[]{:S(2)}) collective-permute-start(bf16[32,6144]{1,0:T(8,128)(2,1)} %copy-done.5), channel_id=1, source_target_pairs={{0,8},{8,16},{16,24},{1,9},{9,17},{17,25},{2,10},{10,18},{18,26},{... | collective-permute-start | bytes 1179656 | tf_op jit(solution)/shard_map/while/body/eval_jaxpr/ppermute | solution.py:14
  189.5 0.8 copy-start.5
  190.3 10.8 %collective-permute-start = (bf16[32,6144]{1,0:T(8,128)(2,1)}, bf16[32,6144]{1,0:T(8,128)(2,1)S(1)}, u32[]{:S(2)}, u32[]{:S(2)}) collective-permute-start(bf16[32,6144]{1,0:T(8,128)(2,1)} %copy-done.5), channel_id=1, source_target_pairs={{0,8},{8,16},{16,24},{1,9},{9,17},{17,25},{2,10},{10,18},{18,26},{... | collective-permute-start | bytes 1179656 | tf_op jit(solution)/shard_map/while/body/eval_jaxpr/ppermute | solution.py:14
  201.1 0.7 copy-start.5
  201.8 17.2 %collective-permute-start = (bf16[32,6144]{1,0:T(8,128)(2,1)}, bf16[32,6144]{1,0:T(8,128)(2,1)S(1)}, u32[]{:S(2)}, u32[]{:S(2)}) collective-permute-start(bf16[32,6144]{1,0:T(8,128)(2,1)} %copy-done.5), channel_id=1, source_target_pairs={{0,8},{8,16},{16,24},{1,9},{9,17},{17,25},{2,10},{10,18},{18,26},{... | collective-permute-start | bytes 1179656 | tf_op jit(solution)/shard_map/while/body/eval_jaxpr/ppermute | solution.py:14
  219.1 0.7 copy-start.5
  219.8 10.8 %collective-permute-start = (bf16[32,6144]{1,0:T(8,128)(2,1)}, bf16[32,6144]{1,0:T(8,128)(2,1)S(1)}, u32[]{:S(2)}, u32[]{:S(2)}) collective-permute-start(bf16[32,6144]{1,0:T(8,128)(2,1)} %copy-done.5), channel_id=1, source_target_pairs={{0,8},{8,16},{16,24},{1,9},{9,17},{17,25},{2,10},{10,18},{18,26},{... | collective-permute-start | bytes 1179656 | tf_op jit(solution)/shard_map/while/body/eval_jaxpr/ppermute | solution.py:14
  230.6 0.7 copy-start.5
  231.4 17.8 %collective-permute-start = (bf16[32,6144]{1,0:T(8,128)(2,1)}, bf16[32,6144]{1,0:T(8,128)(2,1)S(1)}, u32[]{:S(2)}, u32[]{:S(2)}) collective-permute-start(bf16[32,6144]{1,0:T(8,128)(2,1)} %copy-done.5), channel_id=1, source_target_pairs={{0,8},{8,16},{16,24},{1,9},{9,17},{17,25},{2,10},{10,18},{18,26},{... | collective-permute-start | bytes 1179656 | tf_op jit(solution)/shard_map/while/body/eval_jaxpr/ppermute | solution.py:14
  249.2 1.6 copy-start.2
  252.4 3.4 copy-start
  256.6 11.2 %collective-permute-start.1 = (bf16[32,6144]{1,0:T(8,128)(2,1)}, bf16[32,6144]{1,0:T(8,128)(2,1)}, u32[]{:S(2)}, u32[]{:S(2)}) collective-permute-start(bf16[32,6144]{1,0:T(8,128)(2,1)} %get-tuple-element.1024), channel_id=1, source_target_pairs={{8,0},{16,8},{24,16},{9,1},{17,9},{25,17},{10,2},{18,10},{26,18},{... | collective-permute-start | bytes 1179656 | tf_op jit(solution)/shard_map/while/body/eval_jaxpr/ppermute | solution.py:14
  268.6 13.0 %collective-permute-start.1 = (bf16[32,6144]{1,0:T(8,128)(2,1)}, bf16[32,6144]{1,0:T(8,128)(2,1)}, u32[]{:S(2)}, u32[]{:S(2)}) collective-permute-start(bf16[32,6144]{1,0:T(8,128)(2,1)} %get-tuple-element.1024), channel_id=1, source_target_pairs={{8,0},{16,8},{24,16},{9,1},{17,9},{25,17},{10,2},{18,10},{26,18},{... | collective-permute-start | bytes 1179656 | tf_op jit(solution)/shard_map/while/body/eval_jaxpr/ppermute | solution.py:14
  282.4 37.9 %collective-permute-start.1 = (bf16[32,6144]{1,0:T(8,128)(2,1)}, bf16[32,6144]{1,0:T(8,128)(2,1)}, u32[]{:S(2)}, u32[]{:S(2)}) collective-permute-start(bf16[32,6144]{1,0:T(8,128)(2,1)} %get-tuple-element.1024), channel_id=1, source_target_pairs={{8,0},{16,8},{24,16},{9,1},{17,9},{25,17},{10,2},{18,10},{26,18},{... | collective-permute-start | bytes 1179656 | tf_op jit(solution)/shard_map/while/body/eval_jaxpr/ppermute | solution.py:14
  321.5 3.9 copy-start.1
  330.5 10.9 %collective-permute-start.1 = (bf16[32,6144]{1,0:T(8,128)(2,1)}, bf16[32,6144]{1,0:T(8,128)(2,1)}, u32[]{:S(2)}, u32[]{:S(2)}) collective-permute-start(bf16[32,6144]{1,0:T(8,128)(2,1)} %get-tuple-element.1024), channel_id=1, source_target_pairs={{8,0},{16,8},{24,16},{9,1},{17,9},{25,17},{10,2},{18,10},{26,18},{... | collective-permute-start | bytes 1179656 | tf_op jit(solution)/shard_map/while/body/eval_jaxpr/ppermute | solution.py:14
  342.6 3.9 copy-start.1
  351.7 10.8 %collective-permute-start.1 = (bf16[32,6144]{1,0:T(8,128)(2,1)}, bf16[32,6144]{1,0:T(8,128)(2,1)}, u32[]{:S(2)}, u32[]{:S(2)}) collective-permute-start(bf16[32,6144]{1,0:T(8,128)(2,1)} %get-tuple-element.1024), channel_id=1, source_target_pairs={{8,0},{16,8},{24,16},{9,1},{17,9},{25,17},{10,2},{18,10},{26,18},{... | collective-permute-start | bytes 1179656 | tf_op jit(solution)/shard_map/while/body/eval_jaxpr/ppermute | solution.py:14
  363.7 3.9 copy-start.1
  372.7 10.9 %collective-permute-start.1 = (bf16[32,6144]{1,0:T(8,128)(2,1)}, bf16[32,6144]{1,0:T(8,128)(2,1)}, u32[]{:S(2)}, u32[]{:S(2)}) collective-permute-start(bf16[32,6144]{1,0:T(8,128)(2,1)} %get-tuple-element.1024), channel_id=1, source_target_pairs={{8,0},{16,8},{24,16},{9,1},{17,9},{25,17},{10,2},{18,10},{26,18},{... | collective-permute-start | bytes 1179656 | tf_op jit(solution)/shard_map/while/body/eval_jaxpr/ppermute | solution.py:14
  384.8 3.9 copy-start.1
  393.9 10.9 %collective-permute-start.1 = (bf16[32,6144]{1,0:T(8,128)(2,1)}, bf16[32,6144]{1,0:T(8,128)(2,1)}, u32[]{:S(2)}, u32[]{:S(2)}) collective-permute-start(bf16[32,6144]{1,0:T(8,128)(2,1)} %get-tuple-element.1024), channel_id=1, source_target_pairs={{8,0},{16,8},{24,16},{9,1},{17,9},{25,17},{10,2},{18,10},{26,18},{... | collective-permute-start | bytes 1179656 | tf_op jit(solution)/shard_map/while/body/eval_jaxpr/ppermute | solution.py:14
  406.0 3.9 copy-start.1
  415.1 12.0 %collective-permute-start.1 = (bf16[32,6144]{1,0:T(8,128)(2,1)}, bf16[32,6144]{1,0:T(8,128)(2,1)}, u32[]{:S(2)}, u32[]{:S(2)}) collective-permute-start(bf16[32,6144]{1,0:T(8,128)(2,1)} %get-tuple-element.1024), channel_id=1, source_target_pairs={{8,0},{16,8},{24,16},{9,1},{17,9},{25,17},{10,2},{18,10},{26,18},{... | collective-permute-start | bytes 1179656 | tf_op jit(solution)/shard_map/while/body/eval_jaxpr/ppermute | solution.py:14
  428.2 3.9 copy-start.1
  437.3 10.0 %collective-permute-start.1 = (bf16[32,6144]{1,0:T(8,128)(2,1)}, bf16[32,6144]{1,0:T(8,128)(2,1)}, u32[]{:S(2)}, u32[]{:S(2)}) collective-permute-start(bf16[32,6144]{1,0:T(8,128)(2,1)} %get-tuple-element.1024), channel_id=1, source_target_pairs={{8,0},{16,8},{24,16},{9,1},{17,9},{25,17},{10,2},{18,10},{26,18},{... | collective-permute-start | bytes 1179656 | tf_op jit(solution)/shard_map/while/body/eval_jaxpr/ppermute | solution.py:14
  447.3 2.8 copy-start.4
Sparse Core Ops, SparseCore 0:
  9.6 40.9 all-gather.4
  52.2 37.1 all-gather.6
  455.2 67.4 reduce-scatter.1
where the time goes:
time: 534 us; the launch traced here: 532 us
  waiting for transfers between devices  294 us (55%)
  starting transfers between devices  64.6 us (12%)
  matrix products  63 us (12%)
  other arithmetic  48.9 us (9%)
  blocking collectives  27.8 us (5%)
  local copies, waits for them, and re-layouts  19.1 us (4%)
  between operations  13.8 us (3%)
    ppermute x18, waiting for transfers between devices, from_behind(): return lax.ppermute(block, axis, route)  177 us
    ppermute x18, starting transfers between devices, from_behind(): return lax.ppermute(block, axis, route)  64.5 us
    reduce_scatter x1, waiting for transfers between devices, body(): lax.psum_scatter((jnp.concatenate((left_term, right_term), axis=1) * grad...  39.8 us
    all_gather x1, waiting for transfers between devices, body(): lax.all_gather(out_weight[0], 'rep', axis=0, tiled=True)  38.8 us
    all_gather x1, waiting for transfers between devices, body(): lax.all_gather(in_weight[0], 'rep', axis=0, tiled=True)  37.8 us
    dynamic_update_slice x18, other arithmetic, write_slot(): lax.dynamic_update_index_in_dim(holder, content, slot, 0)  32.5 us
    dot_general x6, matrix products, section_forward(): lax.dot_general(activated, out_weight, (((1,), (1,)), ((), ())), preferre...  30.9 us
    psum x1, blocking collectives, body(): grad_gain = lax.psum(gain_total * grad_scale, 'rep')[None]  27.8 us
  transfers between devices with their start and end apart: 21, of which 21 were waited for; matrix products, arithmetic and copies ran while one was open for 1% of the time, Pallas kernels for 0%

commit v1 on v0

--- a/solution.py
+++ b/solution.py
@@ -1,8 +1,11 @@
+import functools
 import math
 
 import jax
 import jax.numpy as jnp
 from jax import lax
+from jax.experimental import pallas as pl
+from jax.experimental.pallas import tpu as pltpu
 from jax.sharding import PartitionSpec as P
 
 norm_epsilon = 1e-05
@@ -57,7 +60,7 @@
     )
 
 
-def body(inputs, cotangent, in_weight, out_weight, norm_gain, lengths):
+def staged_body(inputs, cotangent, in_weight, out_weight, norm_gain, lengths):
     section_count = lax.axis_size("section")
     replicas = lax.axis_size("rep")
     position = lax.axis_index("section")
@@ -161,6 +164,408 @@
     return (grad_in_weight, grad_out_weight, grad_gain, grad_inputs)
 
 
+MESH = pl.DeviceIdType.MESH
+contract_last = (((1,), (1,)), ((), ()))
+contract_rows = (((0,), (0,)), ((), ()))
+carrier = 128
+
+
+def two_halves(column):
+    high = column.astype(jnp.bfloat16).astype(jnp.float32)
+    low = column - high
+    lane = lax.broadcasted_iota(jnp.int32, (column.shape[0], carrier), 1)
+    return jnp.where(lane == 0, high, jnp.where(lane == 1, low, 0.0)).astype(jnp.bfloat16)
+
+
+def window_kernel(
+    sections, replicas, grad_scale,
+    x_ref, c_ref, wg_ref, wo_ref, raw_ref, gain_ref,
+    gin_ref, gout_ref, gain_out_ref, rows_out_ref,
+    hid, up, wgb, wob, fs_out, fs_in, bs_out, bs_in, act, gbi, before, inverse,
+    m_out, n_out, m_in, n_in, gain_own,
+    x_send, x_recv, c_send, c_recv, wg_send, wg_recv, wo_send, wo_recv,
+    fs_send, fs_recv, fg_send, fg_recv, bs_send, bs_recv, bg_send, bg_recv,
+    m_send, m_recv, n_send, n_recv, r_send, r_recv, own_sem, g_send, g_recv,
+):
+    chunk, block = x_ref.shape[1], x_ref.shape[2]
+    rank = wg_ref.shape[1]
+    width = block * replicas
+    sec, rep = lax.axis_index("section"), lax.axis_index("rep")
+
+    def place(r):
+        return pl.ds(pl.multiple_of(r * chunk, 16), chunk)
+
+    def lanes(r):
+        return pl.ds(pl.multiple_of(r * block, 128), block)
+
+    def to_rep(src, dst, send, recv, peer):
+        return pltpu.make_async_remote_copy(
+            src_ref=src, dst_ref=dst, send_sem=send, recv_sem=recv,
+            device_id={"section": sec, "rep": peer}, device_id_type=MESH,
+        )
+
+    def to_sec(src, dst, send, recv, peer):
+        return pltpu.make_async_remote_copy(
+            src_ref=src, dst_ref=dst, send_sem=send, recv_sem=recv,
+            device_id={"section": peer, "rep": rep}, device_id_type=MESH,
+        )
+
+    def each_rep(step):
+        def go(i, carry):
+            step(lax.rem(rep + i, replicas))
+            return carry
+        lax.fori_loop(1, replicas, go, 0)
+
+    def each_sec(step):
+        def go(i, carry):
+            step(lax.rem(sec + i, sections))
+            return carry
+        lax.fori_loop(1, sections, go, 0)
+
+    barrier = pltpu.get_barrier_semaphore()
+    count = sections * replicas
+    mine = sec * replicas + rep
+
+    def greet(i, carry):
+        other = lax.rem(mine + i, count)
+        pl.semaphore_signal(
+            barrier, inc=1,
+            device_id={"section": other // replicas, "rep": lax.rem(other, replicas)},
+            device_id_type=MESH,
+        )
+        return carry
+
+    lax.fori_loop(1, count, greet, 0)
+    pl.semaphore_wait(barrier, count - 1)
+
+    def x_copy(peer, source):
+        return to_rep(x_ref.at[peer], hid.at[0, place(source)], x_send.at[peer], x_recv.at[source], peer)
+
+    def c_copy(peer, source):
+        return to_rep(
+            c_ref.at[peer], up.at[sections, place(source)], c_send.at[peer], c_recv.at[source], peer
+        )
+
+    def wg_copy(peer, source):
+        return to_sec(wg_ref, wgb.at[source], wg_send.at[peer], wg_recv.at[source], peer)
+
+    def wo_copy(peer, source):
+        return to_sec(wo_ref, wob.at[source], wo_send.at[peer], wo_recv.at[source], peer)
+
+    each_rep(lambda peer: x_copy(peer, rep).start())
+    each_sec(lambda peer: wg_copy(peer, sec).start())
+    each_sec(lambda peer: wo_copy(peer, sec).start())
+    hid[0, place(rep)] = x_ref[rep]
+    up[sections, place(rep)] = c_ref[rep]
+    wgb[sec] = wg_ref[...]
+    wob[sec] = wo_ref[...]
+    each_rep(lambda peer: x_copy(peer, peer).wait_recv())
+    each_rep(lambda peer: c_copy(peer, rep).start())
+
+    def fs_copy(s, peer, source):
+        return to_rep(
+            fs_out.at[s, place(peer)], fs_in.at[s, source], fs_send.at[s, peer], fs_recv.at[s, source], peer
+        )
+
+    def bs_copy(s, peer, source):
+        return to_rep(
+            bs_out.at[s, place(peer)], bs_in.at[s, source], bs_send.at[s, peer], bs_recv.at[s, source], peer
+        )
+
+    def fg_copy(s, peer, source):
+        view = act.at[s, place(source)]
+        return to_rep(view, view, fg_send.at[s, peer], fg_recv.at[s, source], peer)
+
+    def bg_copy(s, peer, source):
+        view = gbi.at[s, place(source)]
+        return to_rep(view, view, bg_send.at[s, peer], bg_recv.at[s, source], peer)
+
+    def m_copy(s, source):
+        return to_sec(m_out.at[s], m_in.at[source], m_send.at[s], m_recv.at[source], s)
+
+    def n_copy(s, source):
+        return to_sec(n_out.at[s], n_in.at[source], n_send.at[s], n_recv.at[source], s)
+
+    def forward_send(s):
+        @pl.when(s != sec)
+        def _():
+            wg_copy(s, s).wait_recv()
+
+        hidden = hid[s]
+        partial = jnp.dot(hidden, wgb[s], preferred_element_type=jnp.float32)
+        fs_out[s, :, pl.ds(0, rank)] = partial.astype(jnp.bfloat16)
+        widened = hidden.astype(jnp.float32)
+        fs_out[s, :, pl.ds(rank, carrier)] = two_halves(jnp.sum(widened * widened, axis=1, keepdims=True))
+        each_rep(lambda peer: fs_copy(s, peer, rep).start())
+
+    def summed(copy, out, landing, s):
+        def go(i, total):
+            source = lax.rem(rep + i, replicas)
+            copy(s, source, source).wait_recv()
+            return total + landing[s, source].astype(jnp.float32)
+        return lax.fori_loop(1, replicas, go, out[s, place(rep)].astype(jnp.float32))
+
+    def forward_finish(s):
+        total = summed(fs_copy, fs_out, fs_in, s)
+        square = total[:, rank:rank + 1] + total[:, rank + 1:rank + 2]
+        inv = lax.rsqrt(square / width + norm_epsilon)
+        value = total[:, :rank] * inv
+        before[s] = value
+        inverse[s] = jnp.broadcast_to(inv, (chunk, carrier))
+        act[s, place(rep)] = (value / (1.0 + jnp.exp(-value))).astype(jnp.bfloat16)
+        each_rep(lambda peer: fg_copy(s, peer, rep).start())
+
+    def wait_act(s):
+        each_rep(lambda peer: fg_copy(s, peer, peer).wait_recv())
+
+    def wait_wo(s):
+        @pl.when(s != sec)
+        def _():
+            wo_copy(s, s).wait_recv()
+
+    def backward_send(s):
+        bs_out[s] = jnp.dot(up[s + 1], wob[s], preferred_element_type=jnp.float32).astype(jnp.bfloat16)
+        each_rep(lambda peer: bs_copy(s, peer, rep).start())
+
+    def backward_finish(s):
+        grad_activated = summed(bs_copy, bs_out, bs_in, s)
+        value = before[s]
+        inv = inverse[s][:, :1]
+        sig = 1.0 / (1.0 + jnp.exp(-value))
+        grad_before = grad_activated * sig * (1.0 + value * (1.0 - sig))
+        share = inv * inv * jnp.sum(grad_before * value, axis=1, keepdims=True) / width
+        gbi[s, place(rep), pl.ds(0, rank)] = (grad_before * inv).astype(jnp.bfloat16)
+        gbi[s, place(rep), pl.ds(rank, carrier)] = two_halves(share)
+        each_rep(lambda peer: bg_copy(s, peer, rep).start())
+
+    def upstream_step(s):
+        each_rep(lambda peer: bg_copy(s, peer, peer).wait_recv())
+        grads = gbi[s]
+        tail = grads[:, rank:].astype(jnp.float32)
+        share = tail[:, 0:1] + tail[:, 1:2]
+        spread = lax.dot_general(grads[:, :rank], wgb[s], contract_last, preferred_element_type=jnp.float32)
+        up[s] = (
+            up[s + 1].astype(jnp.float32) + spread - hid[s].astype(jnp.float32) * share
+        ).astype(jnp.bfloat16)
+
+    def rows_copy(s, r, from_s, from_r):
+        return pltpu.make_async_remote_copy(
+            src_ref=up.at[s, place(r)],
+            dst_ref=rows_out_ref.at[place(from_s), lanes(from_r)],
+            send_sem=r_send.at[s, r], recv_sem=r_recv.at[from_s, from_r],
+            device_id={"section": s, "rep": r}, device_id_type=MESH,
+        )
+
+    def own_rows():
+        return pltpu.make_async_copy(
+            up.at[sec, place(rep)], rows_out_ref.at[place(sec), lanes(rep)], own_sem
+        )
+
+    def send_rows(s):
+        each_rep(lambda r: rows_copy(s, r, sec, rep).start())
+
+        @pl.when(s == sec)
+        def _():
+            own_rows().start()
+
+        @pl.when(s != sec)
+        def _():
+            rows_copy(s, rep, sec, rep).start()
+
+    def m_step(s):
+        m_out[s] = lax.dot_general(
+            hid[s], gbi[s, :, pl.ds(0, rank)], contract_rows, preferred_element_type=jnp.float32
+        ).astype(jnp.bfloat16)
+
+        @pl.when(s != sec)
+        def _():
+            m_copy(s, sec).start()
+
+    def n_step(s):
+        n_out[s] = lax.dot_general(
+            up[s + 1], act[s], contract_rows, preferred_element_type=jnp.float32
+        ).astype(jnp.bfloat16)
+
+        @pl.when(s != sec)
+        def _():
+            n_copy(s, sec).start()
+
+    def forward(s, carry):
+        forward_send(s)
+        forward_finish(s)
+        wait_wo(s)
+        wait_act(s)
+        mixed = lax.dot_general(act[s], wob[s], contract_last, preferred_element_type=jnp.float32)
+        hid[s + 1] = (hid[s].astype(jnp.float32) + mixed).astype(jnp.bfloat16)
+        return carry
+
+    lax.fori_loop(0, sections - 1, forward, 0)
+    last = sections - 1
+    forward_send(last)
+    wait_wo(last)
+    each_rep(lambda peer: c_copy(peer, peer).wait_recv())
+    backward_send(last)
+    forward_finish(last)
+    backward_finish(last)
+    wait_act(last)
+    n_step(last)
+    upstream_step(last)
+
+    def backward(i, carry):
+        s = last - i
+        backward_send(s)
+        send_rows(s + 1)
+        m_step(s + 1)
+        n_step(s)
+        backward_finish(s)
+        upstream_step(s)
+        return carry
+
+    lax.fori_loop(1, sections, backward, 0)
+    m_step(0)
+    send_rows(0)
+
+    each_sec(lambda peer: n_copy(sec, peer).wait_recv())
+
+    def add_parts(own, landing):
+        total = own[sec].astype(jnp.float32)
+        for i in range(1, sections):
+            total = total + landing[lax.rem(sec + i, sections)].astype(jnp.float32)
+        return total * grad_scale
+
+    gout_ref[...] = add_parts(n_out, n_in).astype(jnp.bfloat16)
+    each_sec(lambda peer: m_copy(sec, peer).wait_recv())
+    product = add_parts(m_out, m_in)
+    gin_ref[...] = (product * gain_ref[...]).astype(jnp.bfloat16)
+    terms = product * raw_ref[...].astype(jnp.float32)
+    high = terms.astype(jnp.bfloat16)
+    low = (terms - high.astype(jnp.float32)).astype(jnp.bfloat16)
+    ones = jnp.ones((8, rank), jnp.bfloat16)
+    gain_own[...] = lax.dot_general(
+        ones, high, contract_last, preferred_element_type=jnp.float32
+    ) + lax.dot_general(ones, low, contract_last, preferred_element_type=jnp.float32)
+
+    def g_copy(peer, source):
+        return to_rep(
+            gain_own, gain_out_ref.at[:, lanes(source)], g_send.at[peer], g_recv.at[source], peer
+        )
+
+    each_rep(lambda peer: g_copy(peer, rep).start())
+    gain_out_ref[:, lanes(rep)] = gain_own[...]
+
+    def each_section(step):
+        def go(s, carry):
+            step(s)
+            return carry
+        lax.fori_loop(0, sections, go, 0)
+
+    def sent(s):
+        each_rep(lambda peer: fs_copy(s, peer, rep).wait_send())
+        each_rep(lambda peer: fg_copy(s, peer, rep).wait_send())
+        each_rep(lambda peer: bs_copy(s, peer, rep).wait_send())
+        each_rep(lambda peer: bg_copy(s, peer, rep).wait_send())
+        each_rep(lambda peer: rows_copy(s, peer, sec, rep).wait_send())
+        each_rep(lambda peer: rows_copy(sec, peer, s, peer).wait_recv())
+
+        @pl.when(s != sec)
+        def _():
+            rows_copy(s, rep, sec, rep).wait_send()
+            rows_copy(s, rep, s, rep).wait_recv()
+            wg_copy(s, sec).wait_send()
+            wo_copy(s, sec).wait_send()
+            m_copy(s, sec).wait_send()
+            n_copy(s, sec).wait_send()
+
+    each_section(sent)
+    own_rows().wait()
+    each_rep(lambda peer: x_copy(peer, rep).wait_send())
+    each_rep(lambda peer: c_copy(peer, rep).wait_send())
+    each_rep(lambda peer: g_copy(peer, rep).wait_send())
+    each_rep(lambda peer: g_copy(peer, peer).wait_recv())
+
+
+def window_body(inputs, cotangent, in_weight, out_weight, norm_gain, lengths):
+    sections, replicas = lax.axis_size("section"), lax.axis_size("rep")
+    sec, rep = lax.axis_index("section"), lax.axis_index("rep")
+    micro_count, tok_rows, width = inputs.shape
+    block, rank = in_weight.shape[1:]
+    own_rows = micro_count * tok_rows
+    chunk = own_rows // sections
+    rows = chunk * replicas
+    grad_scale = 1.0 / math.sqrt(own_rows * replicas)
+    keep = jnp.arange(tok_rows, dtype=jnp.int32)[None, :] < lengths[0][:, None]
+
+    def part(array):
+        piece = lax.dynamic_slice_in_dim(array.reshape(own_rows, width), sec * chunk, chunk, 0)
+        return piece.reshape(chunk, replicas, block).transpose(1, 0, 2)
+
+    kept = lax.dynamic_slice_in_dim(keep.reshape(own_rows), sec * chunk, chunk, 0)
+    x_parts = part(inputs)
+    c_parts = jnp.where(kept[None, :, None], part(cotangent), jnp.zeros((), jnp.bfloat16))
+    gain = lax.dynamic_slice_in_dim(norm_gain[0], rep * block, block, 0)[:, None]
+    scaled = (in_weight[0].astype(jnp.float32) * gain).astype(jnp.bfloat16)
+    bf, f32 = jnp.bfloat16, jnp.float32
+    dma = pltpu.SemaphoreType.DMA
+    vmem = pl.BlockSpec(memory_space=pltpu.VMEM)
+    wide = rank + carrier
+    grad_in, grad_out, grad_gain, grad_rows = pl.pallas_call(
+        functools.partial(window_kernel, sections, replicas, grad_scale),
+        out_shape=(
+            jax.ShapeDtypeStruct((block, rank), bf),
+            jax.ShapeDtypeStruct((block, rank), bf),
+            jax.ShapeDtypeStruct((8, width), f32),
+            jax.ShapeDtypeStruct((own_rows, width), bf),
+        ),
+        in_specs=[vmem] * 6,
+        out_specs=(vmem, vmem, vmem, pl.BlockSpec(memory_space=pl.ANY)),
+        scratch_shapes=[
+            pltpu.VMEM((sections, rows, block), bf),
+            pltpu.VMEM((sections + 1, rows, block), bf),
+            pltpu.VMEM((sections, block, rank), bf),
+            pltpu.VMEM((sections, block, rank), bf),
+            pltpu.VMEM((sections, rows, wide), bf),
+            pltpu.VMEM((sections, replicas, chunk, wide), bf),
+            pltpu.VMEM((sections, rows, rank), bf),
+            pltpu.VMEM((sections, replicas, chunk, rank), bf),
+            pltpu.VMEM((sections, rows, rank), bf),
+            pltpu.VMEM((sections, rows, wide), bf),
+            pltpu.VMEM((sections, chunk, rank), f32),
+            pltpu.VMEM((sections, chunk, carrier), f32),
+            pltpu.VMEM((sections, block, rank), bf),
+            pltpu.VMEM((sections, block, rank), bf),
+            pltpu.VMEM((sections, block, rank), bf),
+            pltpu.VMEM((sections, block, rank), bf),
+            pltpu.VMEM((8, block), f32),
+            *[dma((replicas,))] * 4,
+            *[dma((sections,))] * 4,
+            *[dma((sections, replicas))] * 8,
+            *[dma((sections,))] * 4,
+            *[dma((sections, replicas))] * 2,
+            dma,
+            *[dma((replicas,))] * 2,
+        ],
+        compiler_params=pltpu.CompilerParams(
+            collective_id=0, has_side_effects=True, vmem_limit_bytes=60 * 1024 * 1024
+        ),
+        name="adapter_window",
+    )(x_parts, c_parts, scaled, out_weight[0], in_weight[0], gain)
+    return (
+        grad_in[None],
+        grad_out[None],
+        grad_gain[:1],
+        grad_rows.reshape(1, micro_count, tok_rows, width),
+    )
+
+
+def body(inputs, cotangent, in_weight, out_weight, norm_gain, lengths):
+    sections = lax.axis_size("section")
+    block, rank = in_weight.shape[1:]
+    own_rows = inputs.shape[0] * inputs.shape[1]
+    aligned = own_rows % (16 * sections) == 0 and block % 128 == 0 and rank % 128 == 0
+    chosen = window_body if aligned else staged_body
+    return chosen(inputs, cotangent, in_weight, out_weight, norm_gain, lengths)
+
+
 def solution(mesh):
     in_specs = (
         P(None, "rep", None),

time: 534 us -> 250 us (0.47)
  waiting for transfers between devices: 294 us -> 0 us
  Pallas kernels: 0 us -> 233 us
  starting transfers between devices: 64.6 us -> 0 us
  matrix products: 63 us -> 0 us
  other arithmetic: 48.9 us -> 3.57 us
  blocking collectives: 27.8 us -> 0 us
  between operations: 13.8 us -> 0.66 us
  local copies, waits for them, and re-layouts: 19.1 us -> 12.4 us
    pallas_call x0 -> x1, Pallas kernels: none -> 233 us  [window_body(): pl.pallas_call(functools.partial(window_kernel, sections, replicas, grad_...]
    ppermute x18 -> x0, waiting for transfers between devices: 177 us -> none  [from_behind(): return lax.ppermute(block, axis, route)]
    all_gather x2 -> x0, waiting for transfers between devices: 76.6 us -> none  [the longest x1 38.8 us: body(): lax.all_gather(out_weight[0], 'rep', axis=0, tiled=True)]
    ppermute x18 -> x0, starting transfers between devices: 64.5 us -> none  [from_behind(): return lax.ppermute(block, axis, route)]
    dot_general x26 -> x0, matrix products: 63 us -> none  [the longest x6 30.9 us: section_forward(): lax.dot_general(activated, out_weight, (((1,), (1,)), ((), ())), preferre...]
    reduce_scatter x1 -> x0, waiting for transfers between devices: 39.8 us -> none  [body(): lax.psum_scatter((jnp.concatenate((left_term, right_term), axis=1) * grad...]
    dynamic_update_slice x18 -> x0, other arithmetic: 32.5 us -> none  [write_slot(): lax.dynamic_update_index_in_dim(holder, content, slot, 0)]
    psum x1 -> x0, blocking collectives: 27.8 us -> none  [body(): grad_gain = lax.psum(gain_total * grad_scale, 'rep')[None]]
  transfers between devices with their start and end apart: 21 -> 0, of which waited for: 21 -> 0; matrix products, arithmetic and copies ran while one was open for 1% -> 0% of each run, Pallas kernels for 0% -> 0%
where the time goes in v1:
time: 250 us; the launch traced here: 249 us
  Pallas kernels  233 us (93%)
  local copies, waits for them, and re-layouts  12.4 us (5%)
  other arithmetic  3.57 us (1%)
    pallas_call x1, Pallas kernels, window_body(): pl.pallas_call(functools.partial(window_kernel, sections, replicas, grad_...  233 us
    unnamed x3, local copies, waits for them, and re-layouts  6.83 us

profile of v1, /device:TPU:0, one launch (start us, length us, event | category | flops | bytes accessed | tf_op | source)
XLA Modules:
  0.0 249.4 jit_solution(14263058547874700256)
XLA Ops:
  0.6 0.7 iota_compare_fusion
  1.4 0.1 lt.32
  1.5 0.1 dynamic_slice.13
  1.5 0.7 dynamic-slice_bitcast_fusion
  2.2 0.9 copy.12.gain_ref
  3.2 1.9 multiply_convert_fusion.wg_ref
  5.1 1.3 constant_dynamic-slice_fusion
  6.4 0.9 fusion.c_ref
  7.3 0.9 copy.17
  8.2 232.8 %adapter_window.1 = (bf16[768,256]{1,0:T(8,128)(2,1)}, bf16[768,256]{1,0:T(8,128)(2,1)}, f32[8,6144]{1,0:T(8,128)}, bf16[192,6144]{1,0:T(8,128)(2,1)}) custom-call(bf16[8,48,768]{2,1,0:T(8,128)(2,1)} %bitcast.28, bf16[8,48,768]{2,1,0:T(8,128)(2,1)} %fusion.c_ref, bf16[768,256]{1,0:T(8,128)(2,1)} %multiply_convert_fusion.wg_ref, bf16[768,256]{1,0:T(8,128)(2,1)} %bitcast.32, ...), custom_call_target="tpu_custom_call" | custom-call | tf_op jit(solution)/shard_map/adapter_window/pallas_call | solution.py:511
  241.0 1.5 slice.3
  242.6 1.8 copy.21
  244.3 1.8 copy.22
  246.1 3.3 %copy.23 = bf16[1,6,32,6144]{3,2,1,0:T(8,128)(2,1)} copy(bf16[1,6,32,6144]{3,2,1,0:T(8,128)(2,1)} %bitcast.27) | data formatting | bytes 4718592

commit v2 on v1

--- a/solution.py
+++ b/solution.py
@@ -181,19 +181,32 @@
     sections, replicas, grad_scale,
     x_ref, c_ref, wg_ref, wo_ref, raw_ref, gain_ref,
     gin_ref, gout_ref, gain_out_ref, rows_out_ref,
-    hid, up, wgb, wob, fs_out, fs_in, bs_out, bs_in, act, gbi, before, inverse,
-    m_out, n_out, m_in, n_in, gain_own,
+    hid, up, wgb, wob, fs_out, fs_pair, fs_mid, fs_in, bs_out, bs_pair, bs_mid, bs_in,
+    act, gbi, before, inverse, m_out, n_out, m_tree, n_tree, m_in, n_in, land, gain_own,
     x_send, x_recv, c_send, c_recv, wg_send, wg_recv, wo_send, wo_recv,
-    fs_send, fs_recv, fg_send, fg_recv, bs_send, bs_recv, bg_send, bg_recv,
-    m_send, m_recv, n_send, n_recv, r_send, r_recv, own_sem, g_send, g_recv,
+    fp_send, fp_recv, bp_send, bp_recv, fs_send, fs_recv, bs_send, bs_recv,
+    fg_send, fg_recv, fh_send, fh_recv, bg_send, bg_recv, bh_send, bh_recv,
+    mt_send, mt_recv, m_send, m_recv, nt_send, nt_recv, n_send, n_recv,
+    r_send, r_recv, q_send, q_recv, own_sem, g_send, g_recv,
 ):
-    chunk, block = x_ref.shape[1], x_ref.shape[2]
+    chunk, block = x_ref.shape[0], x_ref.shape[1] // replicas
     rank = wg_ref.shape[1]
     width = block * replicas
     sec, rep = lax.axis_index("section"), lax.axis_index("rep")
 
+    stops = replicas // 2
+    stop, core = rep // 2, lax.rem(rep, 2)
+    partner = stop * 2 + 1 - core
+    group = stops * chunk
+
+    def spot(i):
+        return pl.ds(pl.multiple_of(i * chunk, 16), chunk)
+
     def place(r):
-        return pl.ds(pl.multiple_of(r * chunk, 16), chunk)
+        return spot(lax.rem(r, 2) * stops + r // 2)
+
+    def half(c):
+        return pl.ds(pl.multiple_of(c * group, 16), group)
 
     def lanes(r):
         return pl.ds(pl.multiple_of(r * block, 128), block)
@@ -215,6 +228,12 @@
             step(lax.rem(rep + i, replicas))
             return carry
         lax.fori_loop(1, replicas, go, 0)
+
+    def each_stop(step):
+        def go(i, carry):
+            step(lax.rem(stop + i, stops))
+            return carry
+        lax.fori_loop(1, stops, go, 0)
 
     def each_sec(step):
         def go(i, carry):
@@ -239,11 +258,11 @@
     pl.semaphore_wait(barrier, count - 1)
 
     def x_copy(peer, source):
-        return to_rep(x_ref.at[peer], hid.at[0, place(source)], x_send.at[peer], x_recv.at[source], peer)
+        return to_rep(x_ref.at[:, lanes(peer)], hid.at[0, place(source)], x_send.at[peer], x_recv.at[source], peer)
 
     def c_copy(peer, source):
         return to_rep(
-            c_ref.at[peer], up.at[sections, place(source)], c_send.at[peer], c_recv.at[source], peer
+            c_ref.at[:, lanes(peer)], up.at[sections, place(source)], c_send.at[peer], c_recv.at[source], peer
         )
 
     def wg_copy(peer, source):
@@ -255,36 +274,178 @@
     each_rep(lambda peer: x_copy(peer, rep).start())
     each_sec(lambda peer: wg_copy(peer, sec).start())
     each_sec(lambda peer: wo_copy(peer, sec).start())
-    hid[0, place(rep)] = x_ref[rep]
-    up[sections, place(rep)] = c_ref[rep]
+    hid[0, place(rep)] = x_ref[:, lanes(rep)]
+    up[sections, place(rep)] = c_ref[:, lanes(rep)]
     wgb[sec] = wg_ref[...]
     wob[sec] = wo_ref[...]
     each_rep(lambda peer: x_copy(peer, peer).wait_recv())
     each_rep(lambda peer: c_copy(peer, rep).start())
 
-    def fs_copy(s, peer, source):
-        return to_rep(
-            fs_out.at[s, place(peer)], fs_in.at[s, source], fs_send.at[s, peer], fs_recv.at[s, source], peer
-        )
-
-    def bs_copy(s, peer, source):
-        return to_rep(
-            bs_out.at[s, place(peer)], bs_in.at[s, source], bs_send.at[s, peer], bs_recv.at[s, source], peer
-        )
-
-    def fg_copy(s, peer, source):
-        view = act.at[s, place(source)]
-        return to_rep(view, view, fg_send.at[s, peer], fg_recv.at[s, source], peer)
-
-    def bg_copy(s, peer, source):
-        view = gbi.at[s, place(source)]
-        return to_rep(view, view, bg_send.at[s, peer], bg_recv.at[s, source], peer)
-
-    def m_copy(s, source):
-        return to_sec(m_out.at[s], m_in.at[source], m_send.at[s], m_recv.at[source], s)
-
-    def n_copy(s, source):
-        return to_sec(n_out.at[s], n_in.at[source], n_send.at[s], n_recv.at[source], s)
+    class Sum:
+        def __init__(self, out, pair, mid, landing, p_send, p_recv, z_send, z_recv):
+            self.refs = out, pair, mid, landing
+            self.sems = p_send, p_recv, z_send, z_recv
+
+        def pair_copy(self, s):
+            out, pair, _, _ = self.refs
+            p_send, p_recv, _, _ = self.sems
+            return to_rep(out.at[s, half(1 - core)], pair.at[s], p_send.at[s], p_recv.at[s], partner)
+
+        def line_copy(self, s, peer, source):
+            _, _, mid, landing = self.refs
+            _, _, z_send, z_recv = self.sems
+            return to_rep(
+                mid.at[s, spot(peer)], landing.at[s, source],
+                z_send.at[s, peer], z_recv.at[s, source], peer * 2 + core,
+            )
+
+        def start(self, s):
+            self.pair_copy(s).start()
+
+        def middle(self, s):
+            out, pair, mid, _ = self.refs
+            self.pair_copy(s).wait_recv()
+            both = out[s, half(core)].astype(jnp.float32) + pair[s].astype(jnp.float32)
+            mid[s] = both.astype(jnp.bfloat16)
+            each_stop(lambda peer: self.line_copy(s, peer, stop).start())
+
+        def finish(self, s):
+            _, _, mid, landing = self.refs
+
+            def go(i, total):
+                source = lax.rem(stop + i, stops)
+                self.line_copy(s, source, source).wait_recv()
+                return total + landing[s, source].astype(jnp.float32)
+            return lax.fori_loop(1, stops, go, mid[s, spot(stop)].astype(jnp.float32))
+
+        def drain(self, s):
+            self.pair_copy(s).wait_send()
+            each_stop(lambda peer: self.line_copy(s, peer, stop).wait_send())
+
+    class Spread:
+        def __init__(self, ref, z_send, z_recv, p_send, p_recv):
+            self.ref = ref
+            self.sems = z_send, z_recv, p_send, p_recv
+
+        def line_copy(self, s, peer, source):
+            z_send, z_recv, _, _ = self.sems
+            view = self.ref.at[s, place(source * 2 + core)]
+            return to_rep(view, view, z_send.at[s, peer], z_recv.at[s, source], peer * 2 + core)
+
+        def pair_copy(self, s, place_of, held):
+            _, _, p_send, p_recv = self.sems
+            view = self.ref.at[s, place(place_of * 2 + held)]
+            return to_rep(view, view, p_send.at[s, place_of], p_recv.at[s, place_of], partner)
+
+        def start(self, s):
+            each_stop(lambda peer: self.line_copy(s, peer, stop).start())
+            self.pair_copy(s, stop, core).start()
+
+        def finish(self, s):
+            def relay(source):
+                self.line_copy(s, source, source).wait_recv()
+                self.pair_copy(s, source, core).start()
+            each_stop(relay)
+
+            def arrive(i, carry):
+                self.pair_copy(s, i, 1 - core).wait_recv()
+                return carry
+            lax.fori_loop(0, stops, arrive, 0)
+
+        def drain(self, s):
+            each_stop(lambda peer: self.line_copy(s, peer, stop).wait_send())
+
+            def gone(i, carry):
+                self.pair_copy(s, i, core).wait_send()
+                return carry
+            lax.fori_loop(0, stops, gone, 0)
+
+    forward_sum = Sum(fs_out, fs_pair, fs_mid, fs_in, fp_send, fp_recv, fs_send, fs_recv)
+    backward_sum = Sum(bs_out, bs_pair, bs_mid, bs_in, bp_send, bp_recv, bs_send, bs_recv)
+    act_spread = Spread(act, fg_send, fg_recv, fh_send, fh_recv)
+    gbi_spread = Spread(gbi, bg_send, bg_recv, bh_send, bh_recv)
+
+    flip_x = sec // 2 * 2 + 1 - lax.rem(sec, 2)
+    flip_y = (1 - sec // 2) * 2 + lax.rem(sec, 2)
+
+    def relation(s):
+        return lax.rem(sec // 2 + s // 2, 2) * 2 + lax.rem(sec + s, 2)
+
+    class Tree:
+        def __init__(self, out, tree, landing, t_send, t_recv, o_send, o_recv):
+            self.refs = out, tree, landing
+            self.sems = t_send, t_recv, o_send, o_recv
+
+        def part(self, i):
+            return pl.ds(i * (block // 2), block // 2)
+
+        def corner_copy(self, s, i):
+            out, tree, _ = self.refs
+            t_send, t_recv, _, _ = self.sems
+            return to_sec(
+                out.at[s, self.part(i)], tree.at[s], t_send.at[s, i], t_recv.at[s], (flip_x, flip_y)[i]
+            )
+
+        def owner_copy(self, s, side, i):
+            out, _, landing = self.refs
+            _, _, o_send, o_recv = self.sems
+            return to_sec(
+                out.at[s, self.part(i)], landing.at[side, self.part(i)],
+                o_send.at[s, i], o_recv.at[side, i], s,
+            )
+
+        def start(self, s):
+            near = relation(s)
+
+            @pl.when(near == 3)
+            def _():
+                self.corner_copy(s, 0).start()
+                self.corner_copy(s, 1).start()
+
+            for side in range(2):
+                @pl.when(near == side + 1)
+                def _():
+                    self.owner_copy(s, side, side).start()
+
+        def relay(self, s):
+            near = relation(s)
+            out, tree, _ = self.refs
+            for side in range(2):
+                @pl.when(near == side + 1)
+                def _():
+                    other = 1 - side
+                    self.corner_copy(s, other).wait_recv()
+                    out[s, self.part(other)] = (
+                        out[s, self.part(other)].astype(jnp.float32) + tree[s].astype(jnp.float32)
+                    ).astype(jnp.bfloat16)
+                    self.owner_copy(s, side, other).start()
+
+        def finish(self):
+            out, _, landing = self.refs
+            for side in range(2):
+                for i in range(2):
+                    self.owner_copy(sec, side, i).wait_recv()
+            total = out[sec].astype(jnp.float32)
+            for side in range(2):
+                total = total + landing[side].astype(jnp.float32)
+            return total * grad_scale
+
+        def drain(self, s):
+            near = relation(s)
+
+            @pl.when(near == 3)
+            def _():
+                self.corner_copy(s, 0).wait_send()
+                self.corner_copy(s, 1).wait_send()
+
+            for side in range(2):
+                @pl.when(near == side + 1)
+                def _():
+                    self.owner_copy(s, side, 0).wait_send()
+                    self.owner_copy(s, side, 1).wait_send()
+
+    m_way = Tree(m_out, m_tree, m_in, mt_send, mt_recv, m_send, m_recv)
+    n_way = Tree(n_out, n_tree, n_in, nt_send, nt_recv, n_send, n_recv)
 
     def forward_send(s):
         @pl.when(s != sec)
@@ -296,27 +457,17 @@
         fs_out[s, :, pl.ds(0, rank)] = partial.astype(jnp.bfloat16)
         widened = hidden.astype(jnp.float32)
         fs_out[s, :, pl.ds(rank, carrier)] = two_halves(jnp.sum(widened * widened, axis=1, keepdims=True))
-        each_rep(lambda peer: fs_copy(s, peer, rep).start())
-
-    def summed(copy, out, landing, s):
-        def go(i, total):
-            source = lax.rem(rep + i, replicas)
-            copy(s, source, source).wait_recv()
-            return total + landing[s, source].astype(jnp.float32)
-        return lax.fori_loop(1, replicas, go, out[s, place(rep)].astype(jnp.float32))
+        forward_sum.start(s)
 
     def forward_finish(s):
-        total = summed(fs_copy, fs_out, fs_in, s)
+        total = forward_sum.finish(s)
         square = total[:, rank:rank + 1] + total[:, rank + 1:rank + 2]
         inv = lax.rsqrt(square / width + norm_epsilon)
         value = total[:, :rank] * inv
         before[s] = value
         inverse[s] = jnp.broadcast_to(inv, (chunk, carrier))
         act[s, place(rep)] = (value / (1.0 + jnp.exp(-value))).astype(jnp.bfloat16)
-        each_rep(lambda peer: fg_copy(s, peer, rep).start())
-
-    def wait_act(s):
-        each_rep(lambda peer: fg_copy(s, peer, peer).wait_recv())
+        act_spread.start(s)
 
     def wait_wo(s):
         @pl.when(s != sec)
@@ -325,10 +476,10 @@
 
     def backward_send(s):
         bs_out[s] = jnp.dot(up[s + 1], wob[s], preferred_element_type=jnp.float32).astype(jnp.bfloat16)
-        each_rep(lambda peer: bs_copy(s, peer, rep).start())
+        backward_sum.start(s)
 
     def backward_finish(s):
-        grad_activated = summed(bs_copy, bs_out, bs_in, s)
+        grad_activated = backward_sum.finish(s)
         value = before[s]
         inv = inverse[s][:, :1]
         sig = 1.0 / (1.0 + jnp.exp(-value))
@@ -336,10 +487,10 @@
         share = inv * inv * jnp.sum(grad_before * value, axis=1, keepdims=True) / width
         gbi[s, place(rep), pl.ds(0, rank)] = (grad_before * inv).astype(jnp.bfloat16)
         gbi[s, place(rep), pl.ds(rank, carrier)] = two_halves(share)
-        each_rep(lambda peer: bg_copy(s, peer, rep).start())
+        gbi_spread.start(s)
 
     def upstream_step(s):
-        each_rep(lambda peer: bg_copy(s, peer, peer).wait_recv())
+        gbi_spread.finish(s)
         grads = gbi[s]
         tail = grads[:, rank:].astype(jnp.float32)
         share = tail[:, 0:1] + tail[:, 1:2]
@@ -348,53 +499,67 @@
             up[s + 1].astype(jnp.float32) + spread - hid[s].astype(jnp.float32) * share
         ).astype(jnp.bfloat16)
 
-    def rows_copy(s, r, from_s, from_r):
-        return pltpu.make_async_remote_copy(
-            src_ref=up.at[s, place(r)],
-            dst_ref=rows_out_ref.at[place(from_s), lanes(from_r)],
-            send_sem=r_send.at[s, r], recv_sem=r_recv.at[from_s, from_r],
-            device_id={"section": s, "rep": r}, device_id_type=MESH,
-        )
-
-    def own_rows():
+    def line_rows(s, r, source):
+        return to_rep(up.at[s, place(r)], land.at[s, source], r_send.at[s, r], r_recv.at[s, source], r)
+
+    def held_rows(s, source, own):
+        return up.at[s, place(rep)] if own else land.at[s, source]
+
+    def plane_rows(s, source, own, from_s):
+        return to_sec(
+            held_rows(s, source, own), rows_out_ref.at[spot(from_s), lanes(source)],
+            q_send.at[s, source], q_recv.at[from_s, source], s,
+        )
+
+    def kept_rows(source, own):
         return pltpu.make_async_copy(
-            up.at[sec, place(rep)], rows_out_ref.at[place(sec), lanes(rep)], own_sem
-        )
-
-    def send_rows(s):
-        each_rep(lambda r: rows_copy(s, r, sec, rep).start())
-
-        @pl.when(s == sec)
-        def _():
-            own_rows().start()
-
-        @pl.when(s != sec)
-        def _():
-            rows_copy(s, rep, sec, rep).start()
+            held_rows(sec, source, own), rows_out_ref.at[spot(sec), lanes(source)], own_sem.at[source]
+        )
+
+    def send_rows(s, first, end):
+        def go(i, carry):
+            r = lax.rem(rep + i, replicas)
+            line_rows(s, r, rep).start()
+            return carry
+        lax.fori_loop(first, end, go, 0)
+
+    def pass_rows(s):
+        def move(source, own):
+            @pl.when(s == sec)
+            def _():
+                kept_rows(source, own).start()
+
+            @pl.when(s != sec)
+            def _():
+                plane_rows(s, source, own, sec).start()
+
+        move(rep, True)
+
+        def go(source):
+            line_rows(s, source, source).wait_recv()
+            move(source, False)
+        each_rep(go)
 
     def m_step(s):
         m_out[s] = lax.dot_general(
             hid[s], gbi[s, :, pl.ds(0, rank)], contract_rows, preferred_element_type=jnp.float32
         ).astype(jnp.bfloat16)
 
-        @pl.when(s != sec)
-        def _():
-            m_copy(s, sec).start()
+        m_way.start(s)
 
     def n_step(s):
         n_out[s] = lax.dot_general(
             up[s + 1], act[s], contract_rows, preferred_element_type=jnp.float32
         ).astype(jnp.bfloat16)
 
-        @pl.when(s != sec)
-        def _():
-            n_copy(s, sec).start()
+        n_way.start(s)
 
     def forward(s, carry):
         forward_send(s)
+        forward_sum.middle(s)
         forward_finish(s)
         wait_wo(s)
-        wait_act(s)
+        act_spread.finish(s)
         mixed = lax.dot_general(act[s], wob[s], contract_last, preferred_element_type=jnp.float32)
         hid[s + 1] = (hid[s].astype(jnp.float32) + mixed).astype(jnp.bfloat16)
         return carry
@@ -405,37 +570,57 @@
     wait_wo(last)
     each_rep(lambda peer: c_copy(peer, peer).wait_recv())
     backward_send(last)
+    forward_sum.middle(last)
+    backward_sum.middle(last)
     forward_finish(last)
     backward_finish(last)
-    wait_act(last)
-    n_step(last)
     upstream_step(last)
+    act_spread.finish(last)
+    middle = replicas // 2
 
     def backward(i, carry):
         s = last - i
         backward_send(s)
-        send_rows(s + 1)
+        backward_sum.middle(s)
+        send_rows(s + 1, 1, middle)
+
+        @pl.when(i == 1)
+        def _():
+            n_step(last)
+
         m_step(s + 1)
         n_step(s)
+
+        @pl.when(i == 2)
+        def _():
+            n_way.relay(last)
+
+        @pl.when(i >= 2)
+        def _():
+            m_way.relay(s + 2)
+            n_way.relay(s + 1)
+
         backward_finish(s)
+        send_rows(s + 1, middle, replicas)
+
+        @pl.when(i >= 2)
+        def _():
+            pass_rows(s + 2)
+
         upstream_step(s)
         return carry
 
     lax.fori_loop(1, sections, backward, 0)
+    send_rows(0, 1, replicas)
     m_step(0)
-    send_rows(0)
-
-    each_sec(lambda peer: n_copy(sec, peer).wait_recv())
-
-    def add_parts(own, landing):
-        total = own[sec].astype(jnp.float32)
-        for i in range(1, sections):
-            total = total + landing[lax.rem(sec + i, sections)].astype(jnp.float32)
-        return total * grad_scale
-
-    gout_ref[...] = add_parts(n_out, n_in).astype(jnp.bfloat16)
-    each_sec(lambda peer: m_copy(sec, peer).wait_recv())
-    product = add_parts(m_out, m_in)
+    n_way.relay(0)
+    m_way.relay(1)
+    m_way.relay(0)
+    pass_rows(1)
+    pass_rows(0)
+
+    gout_ref[...] = n_way.finish().astype(jnp.bfloat16)
+    product = m_way.finish()
     gin_ref[...] = (product * gain_ref[...]).astype(jnp.bfloat16)
     terms = product * raw_ref[...].astype(jnp.float32)
     high = terms.astype(jnp.bfloat16)
@@ -460,24 +645,26 @@
         lax.fori_loop(0, sections, go, 0)
 
     def sent(s):
-        each_rep(lambda peer: fs_copy(s, peer, rep).wait_send())
-        each_rep(lambda peer: fg_copy(s, peer, rep).wait_send())
-        each_rep(lambda peer: bs_copy(s, peer, rep).wait_send())
-        each_rep(lambda peer: bg_copy(s, peer, rep).wait_send())
-        each_rep(lambda peer: rows_copy(s, peer, sec, rep).wait_send())
-        each_rep(lambda peer: rows_copy(sec, peer, s, peer).wait_recv())
+        forward_sum.drain(s)
+        backward_sum.drain(s)
+        act_spread.drain(s)
+        gbi_spread.drain(s)
+        m_way.drain(s)
+        n_way.drain(s)
+        each_rep(lambda peer: line_rows(s, peer, rep).wait_send())
 
         @pl.when(s != sec)
         def _():
-            rows_copy(s, rep, sec, rep).wait_send()
-            rows_copy(s, rep, s, rep).wait_recv()
             wg_copy(s, sec).wait_send()
             wo_copy(s, sec).wait_send()
-            m_copy(s, sec).wait_send()
-            n_copy(s, sec).wait_send()
+            plane_rows(s, rep, True, sec).wait_send()
+            plane_rows(sec, rep, True, s).wait_recv()
+            each_rep(lambda source: plane_rows(s, source, False, sec).wait_send())
+            each_rep(lambda source: plane_rows(sec, source, False, s).wait_recv())
 
     each_section(sent)
-    own_rows().wait()
+    kept_rows(rep, True).wait()
+    each_rep(lambda source: kept_rows(source, False).wait())
     each_rep(lambda peer: x_copy(peer, rep).wait_send())
     each_rep(lambda peer: c_copy(peer, rep).wait_send())
     each_rep(lambda peer: g_copy(peer, rep).wait_send())
@@ -496,18 +683,18 @@
     keep = jnp.arange(tok_rows, dtype=jnp.int32)[None, :] < lengths[0][:, None]
 
     def part(array):
-        piece = lax.dynamic_slice_in_dim(array.reshape(own_rows, width), sec * chunk, chunk, 0)
-        return piece.reshape(chunk, replicas, block).transpose(1, 0, 2)
+        return lax.dynamic_slice_in_dim(array.reshape(own_rows, width), sec * chunk, chunk, 0)
 
     kept = lax.dynamic_slice_in_dim(keep.reshape(own_rows), sec * chunk, chunk, 0)
     x_parts = part(inputs)
-    c_parts = jnp.where(kept[None, :, None], part(cotangent), jnp.zeros((), jnp.bfloat16))
+    c_parts = jnp.where(kept[:, None], part(cotangent), jnp.zeros((), jnp.bfloat16))
     gain = lax.dynamic_slice_in_dim(norm_gain[0], rep * block, block, 0)[:, None]
     scaled = (in_weight[0].astype(jnp.float32) * gain).astype(jnp.bfloat16)
     bf, f32 = jnp.bfloat16, jnp.float32
     dma = pltpu.SemaphoreType.DMA
     vmem = pl.BlockSpec(memory_space=pltpu.VMEM)
     wide = rank + carrier
+    stops = replicas // 2
     grad_in, grad_out, grad_gain, grad_rows = pl.pallas_call(
         functools.partial(window_kernel, sections, replicas, grad_scale),
         out_shape=(
@@ -524,25 +711,29 @@
             pltpu.VMEM((sections, block, rank), bf),
             pltpu.VMEM((sections, block, rank), bf),
             pltpu.VMEM((sections, rows, wide), bf),
-            pltpu.VMEM((sections, replicas, chunk, wide), bf),
+            pltpu.VMEM((sections, rows // 2, wide), bf),
+            pltpu.VMEM((sections, rows // 2, wide), bf),
+            pltpu.VMEM((sections, stops, chunk, wide), bf),
             pltpu.VMEM((sections, rows, rank), bf),
-            pltpu.VMEM((sections, replicas, chunk, rank), bf),
+            pltpu.VMEM((sections, rows // 2, rank), bf),
+            pltpu.VMEM((sections, rows // 2, rank), bf),
+            pltpu.VMEM((sections, stops, chunk, rank), bf),
             pltpu.VMEM((sections, rows, rank), bf),
             pltpu.VMEM((sections, rows, wide), bf),
             pltpu.VMEM((sections, chunk, rank), f32),
             pltpu.VMEM((sections, chunk, carrier), f32),
-            pltpu.VMEM((sections, block, rank), bf),
-            pltpu.VMEM((sections, block, rank), bf),
-            pltpu.VMEM((sections, block, rank), bf),
-            pltpu.VMEM((sections, block, rank), bf),
+            *[pltpu.VMEM((sections, block, rank), bf)] * 2,
+            *[pltpu.VMEM((sections, block // 2, rank), bf)] * 2,
+            *[pltpu.VMEM((2, block, rank), bf)] * 2,
+            pltpu.VMEM((sections, replicas, chunk, block), bf),
             pltpu.VMEM((8, block), f32),
             *[dma((replicas,))] * 4,
             *[dma((sections,))] * 4,
-            *[dma((sections, replicas))] * 8,
             *[dma((sections,))] * 4,
-            *[dma((sections, replicas))] * 2,
-            dma,
-            *[dma((replicas,))] * 2,
+            *[dma((sections, stops))] * 12,
+            *[dma((sections, 2)), dma((sections,)), dma((sections, 2)), dma((2, 2))] * 2,
+            *[dma((sections, replicas))] * 4,
+            *[dma((replicas,))] * 3,
         ],
         compiler_params=pltpu.CompilerParams(
             collective_id=0, has_side_effects=True, vmem_limit_bytes=60 * 1024 * 1024
@@ -562,7 +753,8 @@
     block, rank = in_weight.shape[1:]
     own_rows = inputs.shape[0] * inputs.shape[1]
     aligned = own_rows % (16 * sections) == 0 and block % 128 == 0 and rank % 128 == 0
-    chosen = window_body if aligned else staged_body
+    square = sections == 4 and lax.axis_size("rep") % 2 == 0
+    chosen = window_body if aligned and square else staged_body
     return chosen(inputs, cotangent, in_weight, out_weight, norm_gain, lengths)
 
 

time: 250 us -> 205 us (0.82)
  Pallas kernels: 233 us -> 189 us
    pallas_call x1, Pallas kernels: 233 us -> 189 us  [window_body(): pl.pallas_call(functools.partial(window_kernel, sections, replicas, grad_...]
where the time goes in v2:
time: 205 us; the launch traced here: 204 us
  Pallas kernels  189 us (92%)
  local copies, waits for them, and re-layouts  10.2 us (5%)
  other arithmetic  5.03 us (2%)
    pallas_call x1, Pallas kernels, window_body(): pl.pallas_call(functools.partial(window_kernel, sections, replicas, grad_...  189 us
    unnamed x3, local copies, waits for them, and re-layouts  6.83 us

profile of v2, /device:TPU:0, one launch (start us, length us, event | category | flops | bytes accessed | tf_op | source)
XLA Modules:
  0.0 204.4 jit_solution(841100007419701145)
XLA Ops:
  0.6 0.7 iota_compare_fusion
  1.4 0.1 lt.32
  1.5 0.1 dynamic_slice.13
  1.5 0.7 dynamic-slice_bitcast_fusion
  2.2 0.9 copy.10.gain_ref
  3.2 1.9 multiply_convert_fusion.wg_ref
  5.1 2.4 %dynamic-slice_select_fusion = (bf16[48,6144]{1,0:T(8,128)(2,1)}, bf16[48,6144]{1,0:T(8,128)(2,1)}) fusion(bf16[192,6144]{1,0:T(8,128)(2,1)} %bitcast.16, s32[]{:T(128)S(6)} %select_n.12, pred[48]{0:T(512)(128)(4,1)S(1)} %dynamic_slice.13, bf16[192,6144]{1,0:T(8,128)(2,1)} %bitcast.17), kind=kLoop, calls=%fused_computation.1 | loop fusion | flops 294912 | bytes 2359348 | tf_op jit(solution)/shard_map/jit(_where)/select_n | solution.py:690
  7.5 188.5 %adapter_window.1 = (bf16[768,256]{1,0:T(8,128)(2,1)}, bf16[768,256]{1,0:T(8,128)(2,1)}, f32[8,6144]{1,0:T(8,128)}, bf16[192,6144]{1,0:T(8,128)(2,1)}) custom-call(bf16[48,6144]{1,0:T(8,128)(2,1)} %get-tuple-element.15.x_ref, bf16[48,6144]{1,0:T(8,128)(2,1)} %get-tuple-element.14.c_ref, bf16[768,256]{1,0:T(8,128)(2,1)} %multiply_convert_fusion.wg_ref, ...), custom_call_target="tpu_custom_call" | custom-call | tf_op jit(solution)/shard_map/adapter_window/pallas_call | solution.py:698
  196.0 1.5 slice.3
  197.6 1.8 copy.14
  199.3 1.8 copy.15
  201.1 3.3 %copy.16 = bf16[1,6,32,6144]{3,2,1,0:T(8,128)(2,1)} copy(bf16[1,6,32,6144]{3,2,1,0:T(8,128)(2,1)} %bitcast.11) | data formatting | bytes 4718592

commit v3 on v2

--- a/solution.py
+++ b/solution.py
@@ -182,12 +182,12 @@
     x_ref, c_ref, wg_ref, wo_ref, raw_ref, gain_ref,
     gin_ref, gout_ref, gain_out_ref, rows_out_ref,
     hid, up, wgb, wob, fs_out, fs_pair, fs_mid, fs_in, bs_out, bs_pair, bs_mid, bs_in,
-    act, gbi, before, inverse, m_out, n_out, m_tree, n_tree, m_in, n_in, land, gain_own,
+    act, gbi, before, inverse, m_out, n_out, m_tree, n_tree, m_in, n_in, land, far, gain_own,
     x_send, x_recv, c_send, c_recv, wg_send, wg_recv, wo_send, wo_recv,
     fp_send, fp_recv, bp_send, bp_recv, fs_send, fs_recv, bs_send, bs_recv,
     fg_send, fg_recv, fh_send, fh_recv, bg_send, bg_recv, bh_send, bh_recv,
     mt_send, mt_recv, m_send, m_recv, nt_send, nt_recv, n_send, n_recv,
-    r_send, r_recv, q_send, q_recv, own_sem, g_send, g_recv,
+    r_send, r_recv, q_send, q_recv, v_send, v_recv, w_send, own_sem, g_send, g_recv,
 ):
     chunk, block = x_ref.shape[0], x_ref.shape[1] // replicas
     rank = wg_ref.shape[1]
@@ -198,6 +198,7 @@
     stop, core = rep // 2, lax.rem(rep, 2)
     partner = stop * 2 + 1 - core
     group = stops * chunk
+    middle = replicas // 2
 
     def spot(i):
         return pl.ds(pl.multiple_of(i * chunk, 16), chunk)
@@ -511,6 +512,33 @@
             q_send.at[s, source], q_recv.at[from_s, source], s,
         )
 
+    def corner_rows(s, source, own):
+        side = source // middle
+        slot = lax.rem(source, middle)
+        return to_sec(
+            held_rows(s, source, own), far.at[s, slot], v_send.at[s, source], v_recv.at[s, slot],
+            flip_y + side * (flip_x - flip_y),
+        )
+
+    def onward_rows(s, side, slot):
+        source, origin = side * middle + slot, (flip_y, flip_x)[side]
+        return to_sec(
+            far.at[s, slot], rows_out_ref.at[spot(origin), lanes(source)],
+            w_send.at[s, slot], q_recv.at[origin, source], s,
+        )
+
+    def relay_rows(s):
+        near = relation(s)
+        for side in range(2):
+            @pl.when(near == side + 1)
+            def _():
+                def go(slot, carry):
+                    arrived = to_sec(far.at[s, slot], far.at[s, slot], v_send.at[s, 0], v_recv.at[s, slot], s)
+                    arrived.wait_recv()
+                    onward_rows(s, side, slot).start()
+                    return carry
+                lax.fori_loop(0, middle, go, 0)
+
     def kept_rows(source, own):
         return pltpu.make_async_copy(
             held_rows(sec, source, own), rows_out_ref.at[spot(sec), lanes(source)], own_sem.at[source]
@@ -529,9 +557,15 @@
             def _():
                 kept_rows(source, own).start()
 
-            @pl.when(s != sec)
+            near = relation(s)
+
+            @pl.when((near == 1) | (near == 2))
             def _():
                 plane_rows(s, source, own, sec).start()
+
+            @pl.when(near == 3)
+            def _():
+                corner_rows(s, source, own).start()
 
         move(rep, True)
 
@@ -576,7 +610,6 @@
     backward_finish(last)
     upstream_step(last)
     act_spread.finish(last)
-    middle = replicas // 2
 
     def backward(i, carry):
         s = last - i
@@ -606,6 +639,10 @@
         @pl.when(i >= 2)
         def _():
             pass_rows(s + 2)
+
+        @pl.when(i >= 3)
+        def _():
+            relay_rows(s + 3)
 
         upstream_step(s)
         return carry
@@ -617,7 +654,10 @@
     m_way.relay(1)
     m_way.relay(0)
     pass_rows(1)
+    relay_rows(2)
     pass_rows(0)
+    relay_rows(1)
+    relay_rows(0)
 
     gout_ref[...] = n_way.finish().astype(jnp.bfloat16)
     product = m_way.finish()
@@ -657,10 +697,26 @@
         def _():
             wg_copy(s, sec).wait_send()
             wo_copy(s, sec).wait_send()
-            plane_rows(s, rep, True, sec).wait_send()
             plane_rows(sec, rep, True, s).wait_recv()
-            each_rep(lambda source: plane_rows(s, source, False, sec).wait_send())
             each_rep(lambda source: plane_rows(sec, source, False, s).wait_recv())
+
+        near = relation(s)
+
+        @pl.when(near == 3)
+        def _():
+            corner_rows(s, rep, True).wait_send()
+            each_rep(lambda source: corner_rows(s, source, False).wait_send())
+
+        for side in range(2):
+            @pl.when(near == side + 1)
+            def _():
+                plane_rows(s, rep, True, sec).wait_send()
+                each_rep(lambda source: plane_rows(s, source, False, sec).wait_send())
+
+                def onward(slot, carry):
+                    onward_rows(s, side, slot).wait_send()
+                    return carry
+                lax.fori_loop(0, middle, onward, 0)
 
     each_section(sent)
     kept_rows(rep, True).wait()
@@ -726,17 +782,19 @@
             *[pltpu.VMEM((sections, block // 2, rank), bf)] * 2,
             *[pltpu.VMEM((2, block, rank), bf)] * 2,
             pltpu.VMEM((sections, replicas, chunk, block), bf),
+            pltpu.VMEM((sections, replicas // 2, chunk, block), bf),
             pltpu.VMEM((8, block), f32),
             *[dma((replicas,))] * 4,
             *[dma((sections,))] * 4,
             *[dma((sections,))] * 4,
             *[dma((sections, stops))] * 12,
             *[dma((sections, 2)), dma((sections,)), dma((sections, 2)), dma((2, 2))] * 2,
-            *[dma((sections, replicas))] * 4,
+            *[dma((sections, replicas))] * 5,
+            *[dma((sections, replicas // 2))] * 2,
             *[dma((replicas,))] * 3,
         ],
         compiler_params=pltpu.CompilerParams(
-            collective_id=0, has_side_effects=True, vmem_limit_bytes=60 * 1024 * 1024
+            collective_id=0, has_side_effects=True, vmem_limit_bytes=40 * 1024 * 1024
         ),
         name="adapter_window",
     )(x_parts, c_parts, scaled, out_weight[0], in_weight[0], gain)

time: 205 us -> 195 us (0.951)
  local copies, waits for them, and re-layouts: 10.2 us -> 4.58 us
  Pallas kernels: 189 us -> 185 us
    unnamed x3 -> x7, local copies, waits for them, and re-layouts: 6.83 us -> 2.91 us
    pallas_call x1, Pallas kernels: 189 us -> 185 us  [window_body(): pl.pallas_call(functools.partial(window_kernel, sections, replicas, grad_...]
where the time goes in v3:
time: 195 us; the launch traced here: 194 us
  Pallas kernels  185 us (95%)
  local copies, waits for them, and re-layouts  4.58 us (2%)
  other arithmetic  3.38 us (2%)
    pallas_call x1, Pallas kernels, window_body(): pl.pallas_call(functools.partial(window_kernel, sections, replicas, grad_...  185 us

profile of v3, /device:TPU:0, one launch (start us, length us, event | category | flops | bytes accessed | tf_op | source)
XLA Modules:
  0.0 193.9 jit_solution(7188083251983739133)
XLA Ops:
  0.6 0.0 copy-start
  0.6 0.0 copy-start.1
  0.7 0.8 iota_compare_fusion
  1.5 0.1 lt.32
  1.5 0.1 dynamic_slice.13
  1.6 0.7 dynamic-slice_bitcast_fusion
  2.3 0.2 copy.10.gain_ref
  2.5 1.2 multiply_convert_fusion.wg_ref
  3.7 1.4 dynamic-slice_select_fusion
  5.1 0.0 copy-done
  5.1 0.0 copy-done.1
  5.1 185.3 %adapter_window.1 = (bf16[768,256]{1,0:T(8,128)(2,1)S(1)}, bf16[768,256]{1,0:T(8,128)(2,1)S(1)}, f32[8,6144]{1,0:T(8,128)S(1)}, bf16[192,6144]{1,0:T(8,128)(2,1)S(1)}) custom-call(bf16[48,6144]{1,0:T(8,128)(2,1)S(1)} %get-tuple-element.15.x_ref, bf16[48,6144]{1,0:T(8,128)(2,1)S(1)} %get-tuple-element.14.c_ref, ...), custom_call_target="tpu_custom_call" | custom-call | tf_op jit(solution)/shard_map/adapter_window/pallas_call | solution.py:754
  190.4 0.6 slice.3
  191.1 0.7 copy.14
  191.8 0.7 copy.15
  192.5 1.4 copy.16
Async XLA Ops:
  0.6 4.5 %copy-start = (bf16[1,768,256]{2,1,0:T(8,128)(2,1)S(1)}, bf16[1,768,256]{2,1,0:T(8,128)(2,1)}, u32[]{:S(2)}) copy-start(bf16[1,768,256]{2,1,0:T(8,128)(2,1)} %param.8) | copy-start | bytes 1179652
  0.6 4.5 %copy-start.1 = (bf16[1,768,256]{2,1,0:T(8,128)(2,1)S(1)}, bf16[1,768,256]{2,1,0:T(8,128)(2,1)}, u32[]{:S(2)}) copy-start(bf16[1,768,256]{2,1,0:T(8,128)(2,1)} %param.9) | copy-start | bytes 1179652
